TPU v7x, 256 devices: a whole 4x4x8 slice. The times are simulated.
256 devices in a mesh: ctx: 32 (over y, z_hi, x), tp: 8 (over z_lo, core).
Axes of the slice: x: 4, y: 4, z: 8 (z_hi: 2, z_lo: 4; z = z_hi * 4 + z_lo), core: 2. Of those that a mesh axis runs over, the one named last changes fastest.
Arguments:
- query_feats: bfloat16 [8192, 8192], P('ctx', 'tp'), may hold values from -6 to 6
- key_feats: bfloat16 [8192, 8192], P('ctx', 'tp'), may hold values from -6 to 6
- value_feats: bfloat16 [8192, 8192], P('ctx', 'tp'), may hold values from -6 to 6
- short_taps: float32 [3, 7, 512], P(None, None, 'tp'), may hold values from -2 to 2
- long_filter: bfloat16 [8192, 512], P('ctx', 'tp'), may hold values from -6 to 6
- skip_gain: float32 [8192], P('tp'), may hold values from -1 to 1
- out_grad: bfloat16 [8192, 8192], P('ctx', 'tp'), may hold values from -6 to 6
Outputs:
- mixed_out: bfloat16 [8192, 8192], P('ctx', 'tp')
- grad_query: bfloat16 [8192, 8192], P('ctx', 'tp')
- grad_key: bfloat16 [8192, 8192], P('ctx', 'tp')
- grad_value: bfloat16 [8192, 8192], P('ctx', 'tp')
- grad_filter: bfloat16 [8192, 512], P('ctx', 'tp')
All inputs are finite; a program needn't handle non-finite values.
Results may differ from a plain program's by a relative error of at most 0.0058.
Values may be sent and summed in bfloat16 or wider, within the bound.
No kernel may reach another device: no remote copies, remote signals or barrier semaphores. Data moves between devices by JAX's collectives and lax.ppermute only.
A program may use at most 128 MiB of HBM per device.

v0:
```python
import functools
import math

import jax
import jax.numpy as jnp
from jax import lax
from jax.experimental import pallas as pl
from jax.experimental.pallas import tpu as pltpu
from jax.sharding import PartitionSpec as P

D = 8192
SHORT_GROUPS = 512
GROUP = D // SHORT_GROUPS
TAPS = 7
HALO = 8
LANES = 128
VMEM_LIMIT = 50 * 1024 * 1024

f32 = jnp.float32
bf16 = jnp.bfloat16


def shifted(value, axis, steps):
    count = lax.axis_size(axis)
    initial, last = (max(0, -steps), min(count, count - steps))
    return lax.ppermute(value, axis, [(source, source + steps) for source in range(initial, last)])


def featurize_kernel(q_ref, k_ref, v_ref, g_ref, before_ref, taps_ref, x_ref, qc_ref, kc_ref, vc_ref, ext):
    rows, cols = q_ref.shape

    def conv(which, ref):
        ext[:HALO, :] = before_ref[which].astype(f32)
        ext[HALO:, :] = ref[...].astype(f32)
        total = taps_ref[which, 0:1, :] * ext[HALO : HALO + rows, :]
        for offset in range(1, TAPS):
            total = total + taps_ref[which, offset : offset + 1, :] * ext[HALO - offset : HALO - offset + rows, :]
        return total

    def emit(value, lo):
        owners = x_ref.shape[0]
        x_ref[:, lo : lo + cols // owners, :] = value.T.astype(bf16).reshape(owners, cols // owners, rows)

    half = x_ref.shape[1] // 2
    key_conv = conv(1, k_ref)
    kc_ref[...] = key_conv
    value_conv = conv(2, v_ref)
    vc_ref[...] = value_conv
    emit(key_conv * value_conv, 0)
    query_conv = conv(0, q_ref)
    qc_ref[...] = query_conv
    emit(g_ref[...].astype(f32) * query_conv, half)


def featurize(query, key, value, grad, before, taps_full, n_ctx):
    rows, width = query.shape
    owned = width // n_ctx
    cols = LANES
    steps = width // cols
    tok = pl.BlockSpec((rows, cols), lambda i: (0, i))
    return pl.pallas_call(
        featurize_kernel,
        grid=(steps,),
        in_specs=[
            tok,
            tok,
            tok,
            tok,
            pl.BlockSpec((3, HALO, cols), lambda i: (0, 0, i)),
            pl.BlockSpec((3, TAPS, cols), lambda i: (0, 0, i)),
        ],
        out_specs=[
            pl.BlockSpec((cols // owned, 2 * owned, rows), lambda i: (i, 0, 0)),
            tok,
            tok,
            tok,
        ],
        out_shape=[
            jax.ShapeDtypeStruct((n_ctx, 2 * owned, rows), bf16),
            jax.ShapeDtypeStruct((rows, width), f32),
            jax.ShapeDtypeStruct((rows, width), f32),
            jax.ShapeDtypeStruct((rows, width), f32),
        ],
        scratch_shapes=[pltpu.VMEM((rows + HALO, cols), f32)],
        compiler_params=pltpu.CompilerParams(vmem_limit_bytes=VMEM_LIMIT),
        name="featurize",
    )(query, key, value, grad, before, taps_full)


WIDE = 2048


def shift_right(value, steps):
    return value if steps == 0 else pltpu.roll(value, steps, axis=1)


def shift_left(value, steps):
    return value if steps == 0 else pltpu.roll(value, value.shape[1] - steps, axis=1)


def build_toeplitz(f_ref, fpad, v8, toe):
    length = f_ref.shape[-1]
    fpad[:, :LANES] = jnp.zeros((1, LANES), f32)
    fpad[:, LANES : 2 * LANES] = jnp.zeros((1, LANES), f32)
    fpad[:, 2 * LANES :] = f_ref[0].astype(f32)
    for lo in range(0, length, WIDE):
        wide = jnp.broadcast_to(fpad[:, lo + LANES : lo + 2 * LANES + WIDE], (8, WIDE + LANES))
        row = lax.broadcasted_iota(jnp.int32, wide.shape, 0)
        for bit in (1, 2, 4):
            wide = jnp.where((row & bit) != 0, shift_right(wide, bit), wide)
        v8[:, lo + LANES : lo + LANES + WIDE] = wide[:, LANES:]
    v8[:, :LANES] = jnp.zeros((8, LANES), f32)
    toe[:, :LANES] = jnp.zeros((LANES, LANES), bf16)

    for lo in range(0, length, WIDE):
        wide = v8[:, lo : lo + LANES + WIDE]
        for p in range(0, LANES // 8, 2):
            pair = [shift_right(wide, 8 * (p + i))[:, LANES:] for i in range(2)]
            toe[8 * p : 8 * p + 16, lo + LANES : lo + LANES + WIDE] = jnp.concatenate(pair, axis=0).astype(bf16)


def longconv_kernel(x_ref, f_ref, y_ref, fg_ref, fpad, v8, toe, gpad, zpad, acc, corr, *, scale):
    blocks, _, _, group, size = x_ref.shape
    length = blocks * size
    rows = blocks * group
    batch = 4
    top = batch * group
    build_toeplitz(f_ref, fpad, v8, toe)
    gpad[:top, :] = jnp.zeros((top, size), bf16)
    gpad[top:, :] = x_ref[:, 0, 0].reshape(rows, size)
    zpad[:rows, :] = x_ref[:, 1, 0].reshape(rows, size)
    zpad[rows:, :] = jnp.zeros((zpad.shape[0] - rows, size), bf16)

    u_t = gpad[top:, :].astype(f32).T.astype(bf16)
    half = rows // 2
    for k in range(blocks):
        depth = rows if k < blocks // 2 else half
        corr[:, size * k : size * (k + 1)] = jnp.dot(
            u_t[:, :depth], zpad[group * k : group * k + depth, :], preferred_element_type=f32
        )
    corr[:, length:] = jnp.zeros((size, corr.shape[1] - length), f32)
    for lo in range(0, length, WIDE):
        total = None
        for p in reversed(range(LANES // 8)):
            part = (
                corr[8 * p : 8 * p + 8, lo : lo + WIDE + LANES]
                + corr[LANES + 8 * p : LANES + 8 * p + 8, lo + LANES : lo + WIDE + 2 * LANES]
            )
            total = part if total is None else shift_left(total, 8) + part
        row = lax.broadcasted_iota(jnp.int32, total.shape, 0)
        for bit in (4, 2, 1):
            total = jnp.where((row & bit) != 0, shift_left(total, bit), total)
        fg_ref[0, :, lo : lo + WIDE] = (jnp.sum(total[:, :WIDE], axis=0, keepdims=True) * scale).astype(bf16)

    def toeplitz_rows(k, width):
        base = 2 * k * LANES
        return jnp.concatenate(
            [toe[:, base + LANES : base + LANES + width], toe[:, base : base + width]], axis=0
        )

    left = jnp.concatenate([gpad[top - group * i : top - group * i + rows, :] for i in range(batch)], axis=1)
    for kb in range(blocks // batch):
        first = top * kb
        right = jnp.concatenate([toeplitz_rows(batch * kb + i, size) for i in range(batch)], axis=0)
        part = jnp.dot(left[: rows - first], right, preferred_element_type=f32)
        acc[first:, :] = part if kb == 0 else acc[first:, :] + part
    y_ref[:, 0, 0] = (acc[...] * scale).astype(bf16).reshape(blocks, group, size)

    for kb in range(blocks // batch):
        first = top * kb
        right = toeplitz_rows(batch * kb, batch * size)
        count = rows - first
        left = jnp.concatenate(
            [zpad[first + group * i : first + group * i + count, :] for i in range(batch)], axis=1
        )
        part = lax.dot_general(left, right, (((1,), (1,)), ((), ())), preferred_element_type=f32)
        acc[:count, :] = part if kb == 0 else acc[:count, :] + part
    y_ref[:, 1, 0] = (acc[...] * scale).astype(bf16).reshape(blocks, group, size)


def longconv(x, filt, scale):
    blocks, both, size = x.shape
    groups = filt.shape[0]
    length = blocks * size
    rows = blocks * GROUP
    x5 = x.reshape(blocks, 2, groups, GROUP, size)
    block5 = pl.BlockSpec((blocks, 2, 1, GROUP, size), lambda g: (0, 0, g, 0, 0))
    lag = pl.BlockSpec((1, 1, length), lambda g: (g, 0, 0))
    y5, fgrad = pl.pallas_call(
        functools.partial(longconv_kernel, scale=scale),
        grid=(groups,),
        in_specs=[block5, lag],
        out_specs=[block5, lag],
        out_shape=[
            jax.ShapeDtypeStruct(x5.shape, bf16),
            jax.ShapeDtypeStruct((groups, 1, length), bf16),
        ],
        scratch_shapes=[
            pltpu.VMEM((1, length + 2 * LANES), f32),
            pltpu.VMEM((8, length + LANES), f32),
            pltpu.VMEM((LANES, length + LANES), bf16),
            pltpu.VMEM((rows + 4 * GROUP, size), bf16),
            pltpu.VMEM((rows + rows // 2, size), bf16),
            pltpu.VMEM((rows, size), f32),
            pltpu.VMEM((size, length + 2 * LANES), f32),
        ],
        compiler_params=pltpu.CompilerParams(vmem_limit_bytes=VMEM_LIMIT),
        name="longconv",
    )(x5, filt.reshape(groups, 1, length))
    return y5.reshape(x.shape), fgrad.reshape(groups, length)


def tokens(y_ref, lo, count, lanes):
    owners = y_ref.shape[0]
    return y_ref[:, lo : lo + count, :lanes].astype(f32).reshape(owners * count, lanes).T


def grads(conv, back, qc, kc, vc, grad, skip):
    gated = (kc * vc).astype(bf16).astype(f32)
    grad_mix = (grad * qc).astype(bf16).astype(f32)
    mixed = conv + skip * gated
    grad_gate = back + skip * grad_mix
    return mixed, grad * mixed, grad_gate * vc, grad_gate * kc


def heads_kernel(y_ref, qc_ref, kc_ref, vc_ref, g_ref, skip_ref, out_ref):
    half = y_ref.shape[1] // 2
    conv = tokens(y_ref, 0, half, LANES)[:HALO]
    back = tokens(y_ref, half, half, LANES)[:HALO]
    grad = g_ref[...].astype(f32)[:HALO]
    _, gq, gk, gv = grads(conv, back, qc_ref[...], kc_ref[...], vc_ref[...], grad, skip_ref[...])
    out_ref[0] = gq.astype(bf16)
    out_ref[1] = gk.astype(bf16)
    out_ref[2] = gv.astype(bf16)


def heads(y, qc, kc, vc, grad, skip):
    n_ctx, both, rows = y.shape
    width = qc.shape[1]
    cols = 512
    top = pl.BlockSpec((HALO, cols), lambda i: (0, i))
    return pl.pallas_call(
        heads_kernel,
        grid=(width // cols,),
        in_specs=[
            pl.BlockSpec((cols // (both // 2), both, LANES), lambda i: (i, 0, 0)),
            top,
            top,
            top,
            pl.BlockSpec((2 * HALO, cols), lambda i: (0, i)),
            pl.BlockSpec((1, cols), lambda i: (0, i)),
        ],
        out_specs=pl.BlockSpec((3, HALO, cols), lambda i: (0, 0, i)),
        out_shape=jax.ShapeDtypeStruct((3, HALO, width), bf16),
        compiler_params=pltpu.CompilerParams(vmem_limit_bytes=VMEM_LIMIT),
        name="heads",
    )(y, qc, kc, vc, grad, skip)


def spread_kernel(
    y_ref, qc_ref, kc_ref, vc_ref, g_ref, skip_ref, after_ref, taps_ref, out_ref, gq_ref, gk_ref, gv_ref, ext
):
    rows = qc_ref.shape[0]
    half = y_ref.shape[1] // 2
    conv = tokens(y_ref, 0, half, rows)
    back = tokens(y_ref, half, half, rows)
    query_conv = qc_ref[...]
    mixed, gq, gk, gv = grads(
        conv, back, query_conv, kc_ref[...], vc_ref[...], g_ref[...].astype(f32), skip_ref[...]
    )
    out_ref[...] = (query_conv * mixed).astype(bf16)
    for which, (signal, target) in enumerate(((gq, gq_ref), (gk, gk_ref), (gv, gv_ref))):
        ext[:rows, :] = signal
        ext[rows:, :] = after_ref[which].astype(f32)
        total = taps_ref[which, 0:1, :] * ext[:rows, :]
        for offset in range(1, TAPS):
            total = total + taps_ref[which, offset : offset + 1, :] * ext[offset : offset + rows, :]
        target[...] = total.astype(bf16)


def spread(y, qc, kc, vc, grad, skip, after, taps_full):
    n_ctx, both, rows = y.shape
    width = qc.shape[1]
    cols = LANES
    tok = pl.BlockSpec((rows, cols), lambda i: (0, i))
    return pl.pallas_call(
        spread_kernel,
        grid=(width // cols,),
        in_specs=[
            pl.BlockSpec((cols // (both // 2), both, rows), lambda i: (i, 0, 0)),
            tok,
            tok,
            tok,
            tok,
            pl.BlockSpec((1, cols), lambda i: (0, i)),
            pl.BlockSpec((3, HALO, cols), lambda i: (0, 0, i)),
            pl.BlockSpec((3, TAPS, cols), lambda i: (0, 0, i)),
        ],
        out_specs=[tok] * 4,
        out_shape=[jax.ShapeDtypeStruct((rows, width), bf16)] * 4,
        scratch_shapes=[pltpu.VMEM((rows + HALO, cols), f32)],
        compiler_params=pltpu.CompilerParams(vmem_limit_bytes=VMEM_LIMIT),
        name="spread",
    )(y, qc, kc, vc, grad, skip, after, taps_full)


def body(query_feats, key_feats, value_feats, short_taps, long_filter, skip_gain, out_grad):
    tok_rows, width = query_feats.shape
    group_cols = long_filter.shape[1]
    n_ctx = lax.axis_size("ctx")
    me = lax.axis_index("ctx")
    owned_groups = group_cols // n_ctx
    length = tok_rows * n_ctx
    taps_full = jnp.repeat(short_taps, GROUP, axis=2)
    skip = skip_gain.reshape(1, width)
    rims = jnp.stack([a[tok_rows - HALO :] for a in (query_feats, key_feats, value_feats)])
    before = shifted(rims, "ctx", 1)
    filt_all = lax.all_gather(long_filter.T, "ctx", axis=0, tiled=False)
    filt = lax.dynamic_slice_in_dim(filt_all, me * owned_groups, owned_groups, 1)
    filt = filt.transpose(1, 0, 2).reshape(owned_groups, length)
    x, qc, kc, vc = featurize(query_feats, key_feats, value_feats, out_grad, before, taps_full, n_ctx)
    x = lax.all_to_all(x, "ctx", 0, 0, tiled=True)
    y, fgrad = longconv(x, filt, 1.0 / math.sqrt(length))
    fgrad_all = lax.all_gather(fgrad, "ctx", axis=0, tiled=True)
    grad_filter = lax.dynamic_slice_in_dim(fgrad_all, me * tok_rows, tok_rows, 1).T
    y = lax.all_to_all(y, "ctx", 0, 0, tiled=True)
    after = shifted(heads(y, qc, kc, vc, out_grad, skip), "ctx", -1)
    mixed_out, gq, gk, gv = spread(y, qc, kc, vc, out_grad, skip, after, taps_full)
    return (mixed_out, gq, gk, gv, grad_filter)


def solution(mesh):
    in_specs = (
        P("ctx", "tp"),
        P("ctx", "tp"),
        P("ctx", "tp"),
        P(None, None, "tp"),
        P("ctx", "tp"),
        P("tp"),
        P("ctx", "tp"),
    )
    out_specs = (P("ctx", "tp"),) * 5
    return jax.shard_map(body, mesh=mesh, in_specs=in_specs, out_specs=out_specs, check_vma=False)
```

profile of v0, /device:TPU:38, one launch (start us, length us, event | category | flops | bytes accessed | tf_op | source)
XLA Modules:
  0.0 235.6 jit_solution(17122296032566262559)
XLA Ops:
  7.2 0.0 all-gather.5.cloned.1.call-start
  7.2 0.7 all-gather.5.cloned.1.call-update
  7.9 0.7 slice_bitcast_fusion.2
  8.6 0.7 slice_bitcast_fusion
  9.4 8.1 %collective-permute-start = (bf16[3,8,1024]{2,1,0:T(8,128)(2,1)S(1)}, bf16[3,8,1024]{2,1,0:T(8,128)(2,1)S(1)}, u32[]{:S(2)}, u32[]{:S(2)}) collective-permute-start(bf16[3,8,1024]{2,1,0:T(8,128)(2,1)S(1)} %pad_maximum_fusion), channel_id=1, source_target_pairs={{0,8},{8,16},{16,24},{24,32},{32,40},{40,48},{48,56},{56,64},{64,7... | collective-permute-start | bytes 147464 | tf_op jit(solution)/shard_map/ppermute | solution.py:26
  17.5 0.9 broadcast_in_dim.3
  18.4 0.4 reshape.25.taps_ref
  18.8 0.5 collective-permute-done.before_ref
  19.3 0.0 copy-start
  19.3 1.0 copy-done
  20.3 0.0 copy-start.6
  20.3 1.0 copy-done.6
  21.4 0.0 copy-start.7
  21.4 1.0 copy-done.7
  22.4 0.0 copy-start.8
  22.4 1.0 copy-done.8
  23.5 5.4 %featurize.1 = (bf16[32,64,256]{2,1,0:T(8,128)(2,1)}, f32[256,1024]{1,0:T(8,128)}, f32[256,1024]{1,0:T(8,128)}, f32[256,1024]{1,0:T(8,128)}) custom-call(bf16[256,1024]{1,0:T(8,128)(2,1)S(1)} %copy-done.6, bf16[256,1024]{1,0:T(8,128)(2,1)S(1)} %copy-done.7, bf16[256,1024]{1,0:T(8,128)(2,1)S(1)} %copy-done.8, bf16[256,1024]{1,0:T(8,128)(2,1)S(1)} %copy-done, ...), custom_call_target="tpu_custom_call" | custom-call | tf_op jit(solution)/shard_map/featurize/pallas_call | solution.py:61
  28.9 13.0 %all-to-all-start = ((bf16[32,64,256]{2,1,0:T(8,128)(2,1)}), bf16[32,64,256]{2,1,0:T(8,128)(2,1)S(1)}, u32[]{:S(2)}, u32[]{:S(2)}) async-start(bf16[32,64,256]{2,1,0:T(8,128)(2,1)} %get-tuple-element.15), calls=%async_computation | async-start | bytes 2097152 | tf_op jit(solution)/shard_map/all_to_all | solution.py:322
  42.0 0.0 copy-start.1
  42.0 0.0 copy-start.2
  42.0 0.0 copy-start.9
  42.0 56.7 %all-gather.5.cloned.1.call-done = bf16[2048,256]{1,0:T(8,128)(2,1)} async-done(((bf16[64,256]{1,0:T(8,128)(2,1)}), bf16[2048,256]{1,0:T(8,128)(2,1)}) %all-gather.5.cloned.1.call-update) | async-done | bytes 1048592 | tf_op jit(solution)/shard_map/all_gather | solution.py:318
  98.7 0.9 constant_dynamic-slice_fusion.1
  99.7 0.0 all-to-all-done
  99.7 10.6 %longconv.1 = (bf16[32,2,2,16,256]{4,3,2,1,0:T(8,128)(2,1)S(1)}, bf16[2,1,8192]{2,1,0:T(2,128)(2,1)}) custom-call(bf16[32,2,2,16,256]{4,3,2,1,0:T(8,128)(2,1)S(1)} %bitcast.21, bf16[2,1,8192]{2,1,0:T(2,128)(2,1)S(1)} %reshape_reshape.4.f_ref), custom_call_target="tpu_custom_call" | custom-call | tf_op jit(solution)/shard_map/longconv/pallas_call | solution.py:189
  110.3 0.0 copy-start.5
  110.3 1.0 copy-done.5
  111.3 7.0 %all-to-all-start.1 = ((bf16[32,64,256]{2,1,0:T(8,128)(2,1)}), bf16[32,64,256]{2,1,0:T(8,128)(2,1)S(1)}, u32[]{:S(2)}, u32[]{:S(2)}) async-start(bf16[32,64,256]{2,1,0:T(8,128)(2,1)} %bitcast.22), calls=%async_computation.1 | async-start | bytes 2097152 | tf_op jit(solution)/shard_map/all_to_all | solution.py:326
  118.3 0.0 all-gather.7.cloned.1.call-start
  118.3 0.7 all-gather.7.cloned.1.call-update
  119.0 27.6 %all-to-all-done.1.y_ref = bf16[32,64,256]{2,1,0:T(8,128)(2,1)S(1)} async-done(((bf16[32,64,256]{2,1,0:T(8,128)(2,1)}), bf16[32,64,256]{2,1,0:T(8,128)(2,1)S(1)}, u32[]{:S(2)}, u32[]{:S(2)}) %all-to-all-start.1) | async-done | bytes 1048608 | tf_op jit(solution)/shard_map/all_to_all | solution.py:326
  146.6 0.0 copy-done.1
  146.6 0.0 copy-done.2
  146.6 0.0 copy-done.9
  146.6 0.0 copy-start.3
  146.6 1.2 copy-done.3
  147.8 1.0 heads.1
  148.8 4.1 %collective-permute-start.1 = (bf16[3,8,1024]{2,1,0:T(8,128)(2,1)S(1)}, bf16[3,8,1024]{2,1,0:T(8,128)(2,1)S(1)}, u32[]{:S(2)}, u32[]{:S(2)}) collective-permute-start(bf16[3,8,1024]{2,1,0:T(8,128)(2,1)S(1)} %heads.1), channel_id=1, source_target_pairs={{8,0},{16,8},{24,16},{32,24},{40,32},{48,40},{56,48},{64,56},{72,6... | collective-permute-start | bytes 147464 | tf_op jit(solution)/shard_map/ppermute | solution.py:26
  152.9 66.3 %all-gather.7.cloned.1.call-done = bf16[64,1,8192]{2,1,0:T(2,128)(2,1)} async-done(((bf16[2,1,8192]{2,1,0:T(2,128)(2,1)}), bf16[64,1,8192]{2,1,0:T(2,128)(2,1)}) %all-gather.7.cloned.1.call-update) | async-done | bytes 1048592 | tf_op jit(solution)/shard_map/all_gather | solution.py:324
  219.2 0.9 constant_dynamic-slice_fusion
  220.1 0.6 copy.22
  220.8 0.0 collective-permute-done.1.after_ref
  220.8 0.0 copy-start.4
  220.8 1.2 copy-done.4
  222.0 6.8 %spread.1 = (bf16[256,1024]{1,0:T(8,128)(2,1)}, bf16[256,1024]{1,0:T(8,128)(2,1)}, bf16[256,1024]{1,0:T(8,128)(2,1)}, bf16[256,1024]{1,0:T(8,128)(2,1)}) custom-call(bf16[32,64,256]{2,1,0:T(8,128)(2,1)S(1)} %all-to-all-done.1.y_ref, f32[256,1024]{1,0:T(8,128)S(1)} %copy-done.2, f32[256,1024]{1,0:T(8,128)S(1)} %copy-done.4, ...), custom_call_target="tpu_custom_call" | custom-call | tf_op jit(solution)/shard_map/spread/pallas_call | solution.py:286
  (3 shorter events, 0.0 us)
Async XLA Ops:
  7.2 91.6 %all-gather.5.cloned.1.call-start = ((), (), s32[]{:S(2)}) async-start(), calls=%async_computation.2 | async-start | bytes 1081344 | tf_op jit(solution)/shard_map/all_gather | solution.py:318
  9.4 9.9 %collective-permute-start = (bf16[3,8,1024]{2,1,0:T(8,128)(2,1)S(1)}, bf16[3,8,1024]{2,1,0:T(8,128)(2,1)S(1)}, u32[]{:S(2)}, u32[]{:S(2)}) collective-permute-start(bf16[3,8,1024]{2,1,0:T(8,128)(2,1)S(1)} %pad_maximum_fusion), channel_id=1, source_target_pairs={{0,8},{8,16},{16,24},{24,32},{32,40},{40,48},{48,56},{56,64},{64,7... | collective-permute-start | bytes 147464 | tf_op jit(solution)/shard_map/ppermute | solution.py:26
  19.3 1.0 copy-start
  20.3 1.0 copy-start.6
  21.4 1.0 copy-start.7
  22.4 1.0 copy-start.8
  28.9 70.8 %all-to-all-start = ((bf16[32,64,256]{2,1,0:T(8,128)(2,1)}), bf16[32,64,256]{2,1,0:T(8,128)(2,1)S(1)}, u32[]{:S(2)}, u32[]{:S(2)}) async-start(bf16[32,64,256]{2,1,0:T(8,128)(2,1)} %get-tuple-element.15), calls=%async_computation | async-start | bytes 2097152 | tf_op jit(solution)/shard_map/all_to_all | solution.py:322
  42.0 104.6 %copy-start.1 = (bf16[256,1024]{1,0:T(8,128)(2,1)S(1)}, bf16[256,1024]{1,0:T(8,128)(2,1)}, u32[]{:S(2)}) copy-start(bf16[256,1024]{1,0:T(8,128)(2,1)} %g_ref.5) | copy-start | bytes 1572868
  42.0 104.6 %copy-start.2 = (f32[256,1024]{1,0:T(8,128)S(1)}, f32[256,1024]{1,0:T(8,128)}, u32[]{:S(2)}) copy-start(f32[256,1024]{1,0:T(8,128)} %get-tuple-element.17.qc_ref) | copy-start | bytes 3145732
  42.0 104.6 %copy-start.9 = (f32[1024]{0:T(1024)S(1)}, f32[1024]{0:T(1024)}, u32[]{:S(2)}) copy-start(f32[1024]{0:T(1024)} %param.12) | copy-start | bytes 12292
  110.3 1.0 copy-start.5
  111.3 35.3 %all-to-all-start.1 = ((bf16[32,64,256]{2,1,0:T(8,128)(2,1)}), bf16[32,64,256]{2,1,0:T(8,128)(2,1)S(1)}, u32[]{:S(2)}, u32[]{:S(2)}) async-start(bf16[32,64,256]{2,1,0:T(8,128)(2,1)} %bitcast.22), calls=%async_computation.1 | async-start | bytes 2097152 | tf_op jit(solution)/shard_map/all_to_all | solution.py:326
  118.3 101.0 %all-gather.7.cloned.1.call-start = ((), (), s32[]{:S(2)}) async-start(), calls=%async_computation.3 | async-start | bytes 2162688 | tf_op jit(solution)/shard_map/all_gather | solution.py:324
  146.6 1.2 copy-start.3
  148.8 71.9 %collective-permute-start.1 = (bf16[3,8,1024]{2,1,0:T(8,128)(2,1)S(1)}, bf16[3,8,1024]{2,1,0:T(8,128)(2,1)S(1)}, u32[]{:S(2)}, u32[]{:S(2)}) collective-permute-start(bf16[3,8,1024]{2,1,0:T(8,128)(2,1)S(1)} %heads.1), channel_id=1, source_target_pairs={{8,0},{16,8},{24,16},{32,24},{40,32},{48,40},{56,48},{64,56},{72,6... | collective-permute-start | bytes 147464 | tf_op jit(solution)/shard_map/ppermute | solution.py:26
  220.8 1.2 copy-start.4
Sparse Core Ops, SparseCore 0:
  11.4 87.2 all-gather.4
  123.2 95.9 all-gather.6
where the time goes:
time: 239 us; the launch traced here: 236 us
  waiting for transfers between devices  153 us (64%)
  starting transfers between devices  32.3 us (14%)
  Pallas kernels  23.8 us (10%)
  between operations  14.2 us (6%)
  local copies, waits for them, and re-layouts  12.9 us (5%)
    all_gather x1, waiting for transfers between devices, body(): fgrad_all = lax.all_gather(fgrad, 'ctx', axis=0, tiled=True)  66.3 us
    all_gather x1, waiting for transfers between devices, body(): filt_all = lax.all_gather(long_filter.T, 'ctx', axis=0, tiled=False)  56.7 us
    all_to_all x1, waiting for transfers between devices, body(): y = lax.all_to_all(y, 'ctx', 0, 0, tiled=True)  27.6 us
    all_to_all x1, starting transfers between devices, body(): x = lax.all_to_all(x, 'ctx', 0, 0, tiled=True)  13 us
    ppermute x2, starting transfers between devices, shifted(): lax.ppermute(value, axis, [(source, source + steps) for source in range(i...  12.2 us
    pallas_call x1, Pallas kernels, longconv(): pl.pallas_call(functools.partial(longconv_kernel, scale=scale), grid=(gro...  10.6 us
    unnamed x22, local copies, waits for them, and re-layouts  8.24 us
    all_to_all x1, starting transfers between devices, body(): y = lax.all_to_all(y, 'ctx', 0, 0, tiled=True)  7 us
  transfers between devices with their start and end apart: 6, of which 4 were waited for; matrix products, arithmetic and copies ran while one was open for 2% of the time, Pallas kernels for 3%

commit v1 on v0

v1 whole, which is shorter than its diff:
```python
import functools
import math

import jax
import jax.numpy as jnp
from jax import lax
from jax.experimental import pallas as pl
from jax.experimental.pallas import tpu as pltpu
from jax.sharding import PartitionSpec as P

D = 8192
SHORT_GROUPS = 512
GROUP = D // SHORT_GROUPS
TAPS = 7
HALO = 8
TAIL = 16
SPARE = 8
LANES = 128
VMEM_LIMIT = 30 * 1024 * 1024

f32 = jnp.float32
bf16 = jnp.bfloat16


def shifted(value, axis, steps):
    count = lax.axis_size(axis)
    initial, last = (max(0, -steps), min(count, count - steps))
    return lax.ppermute(value, axis, [(source, source + steps) for source in range(initial, last)])


def featurize_kernel(q_ref, k_ref, v_ref, g_ref, before_ref, taps_ref, f_ref, x_ref, qc_ref, kc_ref, vc_ref, ext):
    rows, cols = q_ref.shape
    owners = x_ref.shape[0]
    half = cols // owners
    owned_groups = f_ref.shape[0] // owners

    def conv(which, ref):
        ext[:HALO, :] = before_ref[which].astype(f32)
        ext[HALO:, :] = ref[...].astype(f32)
        total = taps_ref[which, 0:1, :] * ext[HALO : HALO + rows, :]
        for offset in range(1, TAPS):
            total = total + taps_ref[which, offset : offset + 1, :] * ext[HALO - offset : HALO - offset + rows, :]
        return total

    def emit(value, lo):
        x_ref[:, lo : lo + half, :] = value.T.astype(bf16).reshape(owners, half, rows)

    filt = f_ref[...].astype(f32)
    blank = jnp.zeros((SPARE - owned_groups, rows), f32)
    for owner in range(owners):
        lines = filt[owner * owned_groups : (owner + 1) * owned_groups]
        x_ref[owner, 2 * half :, :] = jnp.concatenate([lines, blank], axis=0).astype(bf16)
    key_conv = conv(1, k_ref)
    kc_ref[...] = key_conv
    value_conv = conv(2, v_ref)
    vc_ref[...] = value_conv
    emit(key_conv * value_conv, 0)
    query_conv = conv(0, q_ref)
    qc_ref[...] = query_conv
    emit(g_ref[...].astype(f32) * query_conv, half)


def in_hbm(*arrays):
    return [pltpu.with_memory_space_constraint(a, pltpu.HBM) for a in arrays]


def featurize(query, key, value, grad, before, taps_full, filt, n_ctx):
    rows, width = query.shape
    chunk = 2 * (width // n_ctx) + SPARE
    owned = width // n_ctx
    cols = LANES
    steps = width // cols
    tok = pl.BlockSpec((rows, cols), lambda i: (0, i))
    return pl.pallas_call(
        featurize_kernel,
        grid=(steps,),
        in_specs=[
            tok,
            tok,
            tok,
            tok,
            pl.BlockSpec((3, HALO, cols), lambda i: (0, 0, i)),
            pl.BlockSpec((3, TAPS, cols), lambda i: (0, 0, i)),
            pl.BlockSpec((cols // GROUP, rows), lambda i: (i, 0)),
        ],
        out_specs=[
            pl.BlockSpec((cols // owned, chunk, rows), lambda i: (i, 0, 0)),
            tok,
            tok,
            tok,
        ],
        out_shape=[
            pltpu.HBM((n_ctx, chunk, rows), bf16),
            jax.ShapeDtypeStruct((rows, width), f32),
            jax.ShapeDtypeStruct((rows, width), f32),
            jax.ShapeDtypeStruct((rows, width), f32),
        ],
        scratch_shapes=[pltpu.VMEM((rows + HALO, cols), f32)],
        compiler_params=pltpu.CompilerParams(vmem_limit_bytes=VMEM_LIMIT),
        name="featurize",
    )(*in_hbm(query, key, value, grad), before, taps_full, filt)


WIDE = 2048


def shift_right(value, steps):
    return value if steps == 0 else pltpu.roll(value, steps, axis=1)


def shift_left(value, steps):
    return value if steps == 0 else pltpu.roll(value, value.shape[1] - steps, axis=1)


def build_toeplitz(fpad, which, length, v8, toe):
    for lo in range(0, length, WIDE):
        wide = jnp.broadcast_to(fpad[pl.ds(which, 1), lo + LANES : lo + 2 * LANES + WIDE], (8, WIDE + LANES))
        row = lax.broadcasted_iota(jnp.int32, wide.shape, 0)
        for bit in (1, 2, 4):
            wide = jnp.where((row & bit) != 0, shift_right(wide, bit), wide)
        v8[:, lo + LANES : lo + LANES + WIDE] = wide[:, LANES:]
    v8[:, :LANES] = jnp.zeros((8, LANES), f32)
    toe[:, :LANES] = jnp.zeros((LANES, LANES), bf16)

    for lo in range(0, length, WIDE):
        wide = v8[:, lo : lo + LANES + WIDE]
        for p in range(0, LANES // 8, 2):
            pair = [shift_right(wide, 8 * (p + i))[:, LANES:] for i in range(2)]
            toe[8 * p : 8 * p + 16, lo + LANES : lo + LANES + WIDE] = jnp.concatenate(pair, axis=0).astype(bf16)


def longconv_kernel(x_ref, y_hbm, fpad, v8, toe, gpad, zpad, acc, corr, fgrad, y_ref, sems, *, scale):
    g = pl.program_id(0)
    blocks, chunk, size = x_ref.shape
    half = (chunk - SPARE) // 2
    length = blocks * size
    rows = blocks * GROUP
    group = GROUP
    batch = 4
    top = batch * group

    @pl.when(g == 0)
    def _():
        fpad[:, : 2 * LANES] = jnp.zeros((SPARE, 2 * LANES), f32)
        for j in range(blocks):
            lo = 2 * LANES + size * j
            fpad[:, lo : lo + size] = x_ref[j, 2 * half :, :].astype(f32)
        fgrad[...] = jnp.zeros_like(fgrad)

    build_toeplitz(fpad, g, length, v8, toe)
    gpad[:top, :] = jnp.zeros((top, size), bf16)
    lines = pl.ds(pl.multiple_of(g * group, group), group)
    back_lines = pl.ds(pl.multiple_of(half + g * group, group), group)
    gpad[top:, :] = x_ref[:, lines, :].reshape(rows, size)
    zpad[:rows, :] = x_ref[:, back_lines, :].reshape(rows, size)
    zpad[rows:, :] = jnp.zeros((zpad.shape[0] - rows, size), bf16)

    u_t = gpad[top:, :].astype(f32).T.astype(bf16)
    near = rows // 2
    for k in range(blocks):
        depth = rows if k < blocks // 2 else near
        corr[:, size * k : size * (k + 1)] = jnp.dot(
            u_t[:, :depth], zpad[group * k : group * k + depth, :], preferred_element_type=f32
        )
    corr[:, length:] = jnp.zeros((size, corr.shape[1] - length), f32)
    for lo in range(0, length, WIDE):
        total = None
        for p in reversed(range(LANES // 8)):
            part = (
                corr[8 * p : 8 * p + 8, lo : lo + WIDE + LANES]
                + corr[LANES + 8 * p : LANES + 8 * p + 8, lo + LANES : lo + WIDE + 2 * LANES]
            )
            total = part if total is None else shift_left(total, 8) + part
        row = lax.broadcasted_iota(jnp.int32, total.shape, 0)
        for bit in (4, 2, 1):
            total = jnp.where((row & bit) != 0, shift_left(total, bit), total)
        fgrad[pl.ds(g, 1), lo : lo + WIDE] = jnp.sum(total[:, :WIDE], axis=0, keepdims=True) * scale

    def toeplitz_rows(k, width):
        base = 2 * k * LANES
        return jnp.concatenate(
            [toe[:, base + LANES : base + LANES + width], toe[:, base : base + width]], axis=0
        )

    left = jnp.concatenate([gpad[top - group * i : top - group * i + rows, :] for i in range(batch)], axis=1)
    for kb in range(blocks // batch):
        first = top * kb
        right = jnp.concatenate([toeplitz_rows(batch * kb + i, size) for i in range(batch)], axis=0)
        part = jnp.dot(left[: rows - first], right, preferred_element_type=f32)
        acc[first:, :] = part if kb == 0 else acc[first:, :] + part
    y_ref[:, lines, :] = (acc[...] * scale).astype(bf16).reshape(blocks, group, size)
    conv_out = pltpu.make_async_copy(y_ref.at[:, lines, :], y_hbm.at[:, lines, :], sems.at[0])
    conv_out.start()

    for kb in range(blocks // batch):
        first = top * kb
        right = toeplitz_rows(batch * kb, batch * size)
        count = rows - first
        left = jnp.concatenate(
            [zpad[first + group * i : first + group * i + count, :] for i in range(batch)], axis=1
        )
        part = lax.dot_general(left, right, (((1,), (1,)), ((), ())), preferred_element_type=f32)
        acc[:count, :] = part if kb == 0 else acc[:count, :] + part
    y_ref[:, back_lines, :] = (acc[...] * scale).astype(bf16).reshape(blocks, group, size)
    back_out = pltpu.make_async_copy(y_ref.at[:, back_lines, :], y_hbm.at[:, back_lines, :], sems.at[1])
    back_out.start()

    @pl.when(g == pl.num_programs(0) - 1)
    def _():
        for j in range(blocks):
            y_ref[j, 2 * half :, :] = fgrad[:, size * j : size * (j + 1)].astype(bf16)
        spare = pl.ds(2 * half, SPARE)
        spare_out = pltpu.make_async_copy(y_ref.at[:, spare, :], y_hbm.at[:, spare, :], sems.at[2])
        spare_out.start()
        spare_out.wait()

    conv_out.wait()
    back_out.wait()


def longconv(x, scale):
    blocks, chunk, size = x.shape
    length = blocks * size
    rows = blocks * GROUP
    groups = (chunk - SPARE) // 2 // GROUP
    return pl.pallas_call(
        functools.partial(longconv_kernel, scale=scale),
        grid=(groups,),
        in_specs=[pl.BlockSpec(memory_space=pltpu.VMEM)],
        out_specs=pl.BlockSpec(memory_space=pltpu.HBM),
        out_shape=pltpu.HBM(x.shape, bf16),
        scratch_shapes=[
            pltpu.VMEM((SPARE, length + 2 * LANES), f32),
            pltpu.VMEM((8, length + LANES), f32),
            pltpu.VMEM((LANES, length + LANES), bf16),
            pltpu.VMEM((rows + 4 * GROUP, size), bf16),
            pltpu.VMEM((rows + rows // 2, size), bf16),
            pltpu.VMEM((rows, size), f32),
            pltpu.VMEM((size, length + 2 * LANES), f32),
            pltpu.VMEM((SPARE, length), f32),
            pltpu.VMEM(x.shape, bf16),
            pltpu.SemaphoreType.DMA((3,)),
        ],
        compiler_params=pltpu.CompilerParams(vmem_limit_bytes=VMEM_LIMIT),
        name="longconv",
    )(x)


def tokens(y_ref, lo, count, lanes):
    owners = y_ref.shape[0]
    return y_ref[:, lo : lo + count, :lanes].astype(f32).reshape(owners * count, lanes).T


def grads(conv, back, qc, kc, vc, grad, skip):
    gated = (kc * vc).astype(bf16).astype(f32)
    grad_mix = (grad * qc).astype(bf16).astype(f32)
    mixed = conv + skip * gated
    grad_gate = back + skip * grad_mix
    return mixed, grad * mixed, grad_gate * vc, grad_gate * kc


def anti_sum(taps_ref, which, ext, count):
    total = taps_ref[which, 0:1, :] * ext[:count, :]
    for offset in range(1, TAPS):
        total = total + taps_ref[which, offset : offset + 1, :] * ext[offset : offset + count, :]
    return total


def heads_kernel(y_ref, qc_ref, kc_ref, vc_ref, g_ref, skip_ref, out_ref):
    half = (y_ref.shape[1] - SPARE) // 2
    conv = tokens(y_ref, 0, half, LANES)[:HALO]
    back = tokens(y_ref, half, half, LANES)[:HALO]
    grad = g_ref[...].astype(f32)[:HALO]
    _, gq, gk, gv = grads(conv, back, qc_ref[...], kc_ref[...], vc_ref[...], grad, skip_ref[...])
    out_ref[0] = gq.astype(bf16)
    out_ref[1] = gk.astype(bf16)
    out_ref[2] = gv.astype(bf16)


def heads(y, qc, kc, vc, grad, skip):
    n_ctx, chunk, rows = y.shape
    width = qc.shape[1]
    cols = 512
    top = pl.BlockSpec((HALO, cols), lambda i: (0, i))
    return pl.pallas_call(
        heads_kernel,
        grid=(width // cols,),
        in_specs=[
            pl.BlockSpec((cols * n_ctx // width, chunk, LANES), lambda i: (i, 0, 0)),
            top,
            top,
            top,
            pl.BlockSpec((2 * HALO, cols), lambda i: (0, i)),
            pl.BlockSpec((1, cols), lambda i: (0, i)),
        ],
        out_specs=pl.BlockSpec((3, HALO, cols), lambda i: (0, 0, i)),
        out_shape=jax.ShapeDtypeStruct((3, HALO, width), bf16),
        compiler_params=pltpu.CompilerParams(vmem_limit_bytes=VMEM_LIMIT),
        name="heads",
    )(y, qc, kc, vc, *in_hbm(grad), skip)


def spread_kernel(
    y_ref, qc_ref, kc_ref, vc_ref, g_ref, skip_ref, taps_ref, out_ref, gq_ref, gk_ref, gv_ref, tail_ref, gf_ref, ext
):
    rows, cols = qc_ref.shape
    owners = y_ref.shape[0]
    half = cols // owners
    owned_groups = gf_ref.shape[0] // owners
    lines = [y_ref[o, 2 * half :, :].astype(f32)[:owned_groups] for o in range(owners)]
    gf_ref[...] = jnp.concatenate(lines, axis=0).astype(bf16)
    conv = tokens(y_ref, 0, half, rows)
    back = tokens(y_ref, half, half, rows)
    query_conv = qc_ref[...]
    mixed, gq, gk, gv = grads(
        conv, back, query_conv, kc_ref[...], vc_ref[...], g_ref[...].astype(f32), skip_ref[...]
    )
    out_ref[...] = (query_conv * mixed).astype(bf16)
    ext[rows:, :] = jnp.zeros((HALO, cols), f32)
    for which, (signal, target) in enumerate(((gq, gq_ref), (gk, gk_ref), (gv, gv_ref))):
        ext[:rows, :] = signal
        tail_ref[which] = signal[rows - TAIL :]
        target[...] = anti_sum(taps_ref, which, ext, rows).astype(bf16)


def spread(y, qc, kc, vc, grad, skip, taps_full):
    n_ctx, chunk, rows = y.shape
    width = qc.shape[1]
    cols = LANES
    tok = pl.BlockSpec((rows, cols), lambda i: (0, i))
    return pl.pallas_call(
        spread_kernel,
        grid=(width // cols,),
        in_specs=[
            pl.BlockSpec((cols * n_ctx // width, chunk, rows), lambda i: (i, 0, 0)),
            tok,
            tok,
            tok,
            tok,
            pl.BlockSpec((1, cols), lambda i: (0, i)),
            pl.BlockSpec((3, TAPS, cols), lambda i: (0, 0, i)),
        ],
        out_specs=[tok] * 4
        + [
            pl.BlockSpec((3, TAIL, cols), lambda i: (0, 0, i)),
            pl.BlockSpec((cols // GROUP, rows), lambda i: (i, 0)),
        ],
        out_shape=[jax.ShapeDtypeStruct((rows, width), bf16)] * 4
        + [jax.ShapeDtypeStruct((3, TAIL, width), f32), jax.ShapeDtypeStruct((width // GROUP, rows), bf16)],
        scratch_shapes=[pltpu.VMEM((rows + HALO, cols), f32)],
        compiler_params=pltpu.CompilerParams(vmem_limit_bytes=VMEM_LIMIT),
        cost_estimate=pl.CostEstimate(flops=12_000_000, bytes_accessed=8_000_000, transcendentals=0),
        name="spread",
    )(y, qc, kc, vc, *in_hbm(grad), skip, taps_full)


def tail_kernel(tail_ref, after_ref, taps_ref, gq_in, gk_in, gv_in, gq_ref, gk_ref, gv_ref, ext):
    for which, target in enumerate((gq_ref, gk_ref, gv_ref)):
        ext[:TAIL, :] = tail_ref[which]
        ext[TAIL:, :] = after_ref[which].astype(f32)
        target[...] = anti_sum(taps_ref, which, ext, TAIL).astype(bf16)


def tail(rims, after, taps_full, gq, gk, gv):
    rows, width = gq.shape
    last = rows // TAIL - 1
    strip = pl.BlockSpec((TAIL, width), lambda i: (last, 0))
    anywhere = pl.BlockSpec(memory_space=pl.ANY)
    return pl.pallas_call(
        tail_kernel,
        grid=(1,),
        in_specs=[
            pl.BlockSpec(rims.shape, lambda i: (0, 0, 0)),
            pl.BlockSpec(after.shape, lambda i: (0, 0, 0)),
            pl.BlockSpec(taps_full.shape, lambda i: (0, 0, 0)),
            anywhere,
            anywhere,
            anywhere,
        ],
        out_specs=[strip] * 3,
        out_shape=[jax.ShapeDtypeStruct(gq.shape, bf16)] * 3,
        scratch_shapes=[pltpu.VMEM((TAIL + HALO, width), f32)],
        input_output_aliases={3: 0, 4: 1, 5: 2},
        compiler_params=pltpu.CompilerParams(vmem_limit_bytes=VMEM_LIMIT),
        name="tail",
    )(rims, after, taps_full, gq, gk, gv)


def body(query_feats, key_feats, value_feats, short_taps, long_filter, skip_gain, out_grad):
    tok_rows, width = query_feats.shape
    n_ctx = lax.axis_size("ctx")
    length = tok_rows * n_ctx
    taps_full = jnp.repeat(short_taps, GROUP, axis=2)
    skip = skip_gain.reshape(1, width)
    rims = jnp.stack([a[tok_rows - HALO :] for a in (query_feats, key_feats, value_feats)])
    before = shifted(rims, "ctx", 1)
    x, qc, kc, vc = featurize(query_feats, key_feats, value_feats, out_grad, before, taps_full, long_filter.T, n_ctx)
    x = lax.all_to_all(x, "ctx", 0, 0, tiled=True)
    y = longconv(x, 1.0 / math.sqrt(length))
    y = lax.all_to_all(y, "ctx", 0, 0, tiled=True)
    after = shifted(heads(y, qc, kc, vc, out_grad, skip), "ctx", -1)
    mixed_out, gq, gk, gv, rims, gf = spread(y, qc, kc, vc, out_grad, skip, taps_full)
    gq, gk, gv = tail(rims, after, taps_full, gq, gk, gv)
    return (mixed_out, gq, gk, gv, gf.T)


def solution(mesh):
    in_specs = (
        P("ctx", "tp"),
        P("ctx", "tp"),
        P("ctx", "tp"),
        P(None, None, "tp"),
        P("ctx", "tp"),
        P("tp"),
        P("ctx", "tp"),
    )
    out_specs = (P("ctx", "tp"),) * 5
    return jax.shard_map(body, mesh=mesh, in_specs=in_specs, out_specs=out_specs, check_vma=False)
```

time: 239 us -> 124 us (0.52)
  waiting for transfers between devices: 153 us -> 3.16 us
  blocking collectives: 0 us -> 78.2 us
  starting transfers between devices: 32.3 us -> 10.8 us
  between operations: 14.2 us -> 0.69 us
  local copies, waits for them, and re-layouts: 12.9 us -> 2.78 us
  Pallas kernels: 23.8 us -> 26.7 us
    all_gather x2 -> x0, waiting for transfers between devices: 123 us -> none  [the longest x1 66.3 us: body(): fgrad_all = lax.all_gather(fgrad, 'ctx', axis=0, tiled=True)]
    all_to_all x0 -> x2, blocking collectives: none -> 78.2 us  [the longest x1 45.4 us: body(): x = lax.all_to_all(x, 'ctx', 0, 0, tiled=True)]
    all_to_all x2 -> x0, waiting for transfers between devices: 27.6 us -> none  [the longest x1 27.6 us: body(): y = lax.all_to_all(y, 'ctx', 0, 0, tiled=True)]
    all_to_all x2 -> x0, starting transfers between devices: 20 us -> none  [the longest x1 13 us: body(): x = lax.all_to_all(x, 'ctx', 0, 0, tiled=True)]
    unnamed x22 -> x4, local copies, waits for them, and re-layouts: 8.24 us -> 0.01 us
    ppermute x2, waiting for transfers between devices: 0.5 us -> 3.16 us  [shifted(): lax.ppermute(value, axis, [(source, source + steps) for source in range(i...]
  transfers between devices with their start and end apart: 6 -> 2, of which waited for: 4 -> 2; matrix products, arithmetic and copies ran while one was open for 2% -> 1% of each run, Pallas kernels for 3% -> 5%
where the time goes in v1:
time: 124 us; the launch traced here: 122 us
  blocking collectives  78.2 us (63%)
  Pallas kernels  26.7 us (22%)
  starting transfers between devices  10.8 us (9%)
  waiting for transfers between devices  3.16 us (3%)
  local copies, waits for them, and re-layouts  2.78 us (2%)
    all_to_all x1, blocking collectives, body(): x = lax.all_to_all(x, 'ctx', 0, 0, tiled=True)  45.4 us
    all_to_all x1, blocking collectives, body(): y = lax.all_to_all(y, 'ctx', 0, 0, tiled=True)  32.8 us
    pallas_call x1, Pallas kernels, longconv(): pl.pallas_call(functools.partial(longconv_kernel, scale=scale), grid=(gro...  11.1 us
    ppermute x2, starting transfers between devices, shifted(): lax.ppermute(value, axis, [(source, source + steps) for source in range(i...  10.8 us
    pallas_call x1, Pallas kernels, featurize(): pl.pallas_call(featurize_kernel, grid=(steps,), in_specs=[tok, tok, tok,...  7.06 us
    pallas_call x1, Pallas kernels, spread(): pl.pallas_call(spread_kernel, grid=(width // cols,), in_specs=[pl.BlockSp...  6.62 us
    ppermute x2, waiting for transfers between devices, shifted(): lax.ppermute(value, axis, [(source, source + steps) for source in range(i...  3.16 us
  transfers between devices with their start and end apart: 2, of which 2 were waited for; matrix products, arithmetic and copies ran while one was open for 1% of the time, Pallas kernels for 5%

profile of v1, /device:TPU:38, one launch (start us, length us, event | category | flops | bytes accessed | tf_op | source)
XLA Modules:
  0.0 122.3 jit_solution(12375507444136133187)
XLA Ops:
  0.6 0.0 copy-start
  0.6 0.7 slice_bitcast_fusion.2
  1.4 0.7 slice_bitcast_fusion
  2.1 8.1 %collective-permute-start = (bf16[3,8,1024]{2,1,0:T(8,128)(2,1)S(1)}, bf16[3,8,1024]{2,1,0:T(8,128)(2,1)S(1)}, u32[]{:S(2)}, u32[]{:S(2)}) collective-permute-start(bf16[3,8,1024]{2,1,0:T(8,128)(2,1)S(1)} %pad_maximum_fusion), channel_id=1, source_target_pairs={{0,8},{8,16},{16,24},{24,32},{32,40},{40,48},{48,56},{56,64},{64,7... | collective-permute-start | bytes 147464 | tf_op jit(solution)/shard_map/ppermute | solution.py:28
  10.2 0.9 broadcast_in_dim.3
  11.2 0.4 reshape.16.taps_ref
  11.5 0.5 collective-permute-done.before_ref
  12.0 0.0 copy-done
  12.1 7.1 %featurize.1 = (bf16[32,72,256]{2,1,0:T(8,128)(2,1)}, f32[256,1024]{1,0:T(8,128)S(1)}, f32[256,1024]{1,0:T(8,128)S(1)}, f32[256,1024]{1,0:T(8,128)S(1)}) custom-call(bf16[256,1024]{1,0:T(8,128)(2,1)} %q_ref.1, bf16[256,1024]{1,0:T(8,128)(2,1)} %k_ref.1, bf16[256,1024]{1,0:T(8,128)(2,1)} %v_ref.1, bf16[256,1024]{1,0:T(8,128)(2,1)} %g_ref.5, ...), custom_call_target="tpu_custom_call" | custom-call | tf_op jit(solution)/shard_map/featurize/pallas_call | solution.py:74
  19.1 45.4 %all_to_all.10.x_ref = bf16[32,72,256]{2,1,0:T(8,128)(2,1)S(1)} all-to-all(bf16[32,72,256]{2,1,0:T(8,128)(2,1)} %get-tuple-element.18), channel_id=1, replica_groups=mesh['ctx'=32,'tp'=8] {'ctx'}, dimensions={0} | all-to-all | bytes 2359296 | tf_op jit(solution)/shard_map/all_to_all | solution.py:398
  64.5 11.1 %longconv.1 = bf16[32,72,256]{2,1,0:T(8,128)(2,1)} custom-call(bf16[32,72,256]{2,1,0:T(8,128)(2,1)S(1)} %all_to_all.10.x_ref), custom_call_target="tpu_custom_call" | custom-call | tf_op jit(solution)/shard_map/longconv/pallas_call | solution.py:226
  75.6 0.0 copy-start.1
  75.6 32.8 %all_to_all.11.y_ref = bf16[32,72,256]{2,1,0:T(8,128)(2,1)S(1)} all-to-all(bf16[32,72,256]{2,1,0:T(8,128)(2,1)} %longconv.1), channel_id=1, replica_groups=mesh['ctx'=32,'tp'=8] {'ctx'}, dimensions={0} | all-to-all | bytes 2359296 | tf_op jit(solution)/shard_map/all_to_all | solution.py:400
  108.4 0.0 copy-done.1
  108.4 1.0 heads.1
  109.4 2.7 %collective-permute-start.1 = (bf16[3,8,1024]{2,1,0:T(8,128)(2,1)S(1)}, bf16[3,8,1024]{2,1,0:T(8,128)(2,1)S(1)}, u32[]{:S(2)}, u32[]{:S(2)}) collective-permute-start(bf16[3,8,1024]{2,1,0:T(8,128)(2,1)S(1)} %heads.1), channel_id=1, source_target_pairs={{8,0},{16,8},{24,16},{32,24},{40,32},{48,40},{56,48},{64,56},{72,6... | collective-permute-start | bytes 147464 | tf_op jit(solution)/shard_map/ppermute | solution.py:28
  112.2 6.6 %spread.1 = (bf16[256,1024]{1,0:T(8,128)(2,1)}, bf16[256,1024]{1,0:T(8,128)(2,1)}, bf16[256,1024]{1,0:T(8,128)(2,1)}, bf16[256,1024]{1,0:T(8,128)(2,1)}, f32[3,1...) custom-call(bf16[32,72,256]{2,1,0:T(8,128)(2,1)S(1)} %all_to_all.11.y_ref, f32[256,1024]{1,0:T(8,128)S(1)} %get-tuple-element.19.qc_ref, ...), custom_call_target="tpu_custom_call" | custom-call | flops 12000000 | bytes 8000000 | tf_op jit(solution)/shard_map/spread/pallas_call | solution.py:331
  118.8 2.7 %collective-permute-done.1.after_ref = bf16[3,8,1024]{2,1,0:T(8,128)(2,1)S(1)} collective-permute-done((bf16[3,8,1024]{2,1,0:T(8,128)(2,1)S(1)}, bf16[3,8,1024]{2,1,0:T(8,128)(2,1)S(1)}, u32[]{:S(2)}, u32[]{:S(2)}) %collective-permute-start.1) | collective-permute-done | bytes 49184 | tf_op jit(solution)/shard_map/ppermute | solution.py:28
  121.4 0.9 tail.1
  (1 shorter events, 0.0 us)
Async XLA Ops:
  0.6 11.4 %copy-start = (bf16[256,64]{0,1:T(8,128)(2,1)S(1)}, bf16[256,64]{0,1:T(8,128)(2,1)}, u32[]{:S(2)}) copy-start(bf16[256,64]{0,1:T(8,128)(2,1)} %param.11) | copy-start | bytes 98308
  2.1 9.9 %collective-permute-start = (bf16[3,8,1024]{2,1,0:T(8,128)(2,1)S(1)}, bf16[3,8,1024]{2,1,0:T(8,128)(2,1)S(1)}, u32[]{:S(2)}, u32[]{:S(2)}) collective-permute-start(bf16[3,8,1024]{2,1,0:T(8,128)(2,1)S(1)} %pad_maximum_fusion), channel_id=1, source_target_pairs={{0,8},{8,16},{16,24},{24,32},{32,40},{40,48},{48,56},{56,64},{64,7... | collective-permute-start | bytes 147464 | tf_op jit(solution)/shard_map/ppermute | solution.py:28
  75.6 32.8 %copy-start.1 = (f32[1024]{0:T(1024)S(1)}, f32[1024]{0:T(1024)}, u32[]{:S(2)}) copy-start(f32[1024]{0:T(1024)} %param.12) | copy-start | bytes 12292
  109.4 12.0 %collective-permute-start.1 = (bf16[3,8,1024]{2,1,0:T(8,128)(2,1)S(1)}, bf16[3,8,1024]{2,1,0:T(8,128)(2,1)S(1)}, u32[]{:S(2)}, u32[]{:S(2)}) collective-permute-start(bf16[3,8,1024]{2,1,0:T(8,128)(2,1)S(1)} %heads.1), channel_id=1, source_target_pairs={{8,0},{16,8},{24,16},{32,24},{40,32},{48,40},{56,48},{64,56},{72,6... | collective-permute-start | bytes 147464 | tf_op jit(solution)/shard_map/ppermute | solution.py:28

commit v2 on v1

v2 whole, which is shorter than its diff:
```python
import functools
import math

import jax
import jax.numpy as jnp
from jax import lax
from jax.experimental import pallas as pl
from jax.experimental.pallas import tpu as pltpu
from jax.sharding import PartitionSpec as P

D = 8192
SHORT_GROUPS = 512
GROUP = D // SHORT_GROUPS
TAPS = 7
HALO = 8
TAIL = 16
COLS = 256
CHUNK = 64
SPARE = 8
LANES = 128
VMEM_LIMIT = 26 * 1024 * 1024

f32 = jnp.float32
bf16 = jnp.bfloat16


def shifted(value, axis, steps):
    count = lax.axis_size(axis)
    initial, last = (max(0, -steps), min(count, count - steps))
    return lax.ppermute(value, axis, [(source, source + steps) for source in range(initial, last)])


def rims_kernel(q_ref, k_ref, v_ref, out_ref):
    for which, ref in enumerate((q_ref, k_ref, v_ref)):
        out_ref[which] = ref[...].astype(f32)[HALO:].astype(bf16)


def last_rows(query, key, value):
    rows, width = query.shape
    last = rows // TAIL - 1
    strip = pl.BlockSpec((TAIL, width), lambda i: (last, 0))
    return pl.pallas_call(
        rims_kernel,
        grid=(1,),
        in_specs=[strip] * 3,
        out_specs=pl.BlockSpec((3, HALO, width), lambda i: (0, 0, 0)),
        out_shape=jax.ShapeDtypeStruct((3, HALO, width), bf16),
        compiler_params=pltpu.CompilerParams(vmem_limit_bytes=VMEM_LIMIT),
        name="rims",
    )(*in_hbm(query, key, value))


def tap_rows(taps_ref, which, lanes):
    return [
        jnp.broadcast_to(taps_ref[HALO * which + j : HALO * which + j + 1, lanes], (8, LANES)) for j in range(TAPS)
    ]


def weighted(taps, pieces):
    total = None
    for tap, piece in zip(taps, pieces):
        term = piece.reshape(piece.shape[0] // 8, 8, LANES) * tap[None]
        total = term if total is None else total + term
    return total.reshape(-1, LANES)


def featurize_kernel(
    q_ref, k_ref, v_ref, g_ref, before_ref, taps_ref, f_ref, x_ref, qc_ref, kc_ref, vc_ref, wide_ref, wide, ext, gated, mix
):
    rows, cols = q_ref.shape
    owners = x_ref.shape[0]
    half = cols // owners
    owned_groups = f_ref.shape[0] // owners
    step = pl.program_id(0)

    @pl.when(step == 0)
    def _():
        groups = taps_ref.shape[2]
        shape = (groups, wide.shape[1])
        spot = lax.broadcasted_iota(jnp.int32, shape, 1) // GROUP == lax.broadcasted_iota(jnp.int32, shape, 0)
        for which in range(3):
            wide[HALO * which : HALO * which + TAPS, :] = jnp.dot(
                taps_ref[which], spot.astype(f32), precision=lax.Precision.HIGHEST, preferred_element_type=f32
            )
            wide[HALO * which + TAPS : HALO * (which + 1), :] = jnp.zeros((HALO - TAPS, wide.shape[1]), f32)

    wide_ref[...] = wide[:, pl.ds(pl.multiple_of(step * cols, cols), cols)]
    for which, ref in enumerate((q_ref, k_ref, v_ref)):
        ext[which, :HALO, :] = before_ref[which].astype(f32)
        ext[which, HALO:, :] = ref[...].astype(f32)
    for left in range(0, cols, LANES):
        lanes = slice(left, left + LANES)
        taps = [tap_rows(wide_ref, which, lanes) for which in range(3)]
        for lo in range(0, rows, CHUNK):
            part = slice(lo, lo + CHUNK)

            def conv(which):
                first = HALO + lo
                return weighted(taps[which], [ext[which, first - j : first - j + CHUNK, lanes] for j in range(TAPS)])

            key_conv = conv(1)
            kc_ref[part, lanes] = key_conv
            value_conv = conv(2)
            vc_ref[part, lanes] = value_conv
            gated[part, lanes] = (key_conv * value_conv).astype(bf16)
            query_conv = conv(0)
            qc_ref[part, lanes] = query_conv
            mix[part, lanes] = (g_ref[part, lanes].astype(f32) * query_conv).astype(bf16)
    x_ref[:, :half, :] = gated[...].T.reshape(owners, half, rows)
    x_ref[:, half : 2 * half, :] = mix[...].T.reshape(owners, half, rows)
    filt = f_ref[...].astype(f32)
    blank = jnp.zeros((SPARE - owned_groups, rows), f32)
    for owner in range(owners):
        lines = filt[owner * owned_groups : (owner + 1) * owned_groups]
        x_ref[owner, 2 * half :, :] = jnp.concatenate([lines, blank], axis=0).astype(bf16)


def in_hbm(*arrays):
    return [pltpu.with_memory_space_constraint(a, pltpu.HBM) for a in arrays]


def featurize(query, key, value, grad, before, short_taps, filt, n_ctx):
    rows, width = query.shape
    owned = width // n_ctx
    chunk = 2 * owned + SPARE
    cols = COLS
    tok = pl.BlockSpec((rows, cols), lambda i: (0, i))
    return pl.pallas_call(
        featurize_kernel,
        grid=(width // cols,),
        in_specs=[
            tok,
            tok,
            tok,
            tok,
            pl.BlockSpec((3, HALO, cols), lambda i: (0, 0, i)),
            pl.BlockSpec(short_taps.shape, lambda i: (0, 0, 0)),
            pl.BlockSpec((cols // GROUP, rows), lambda i: (i, 0)),
        ],
        out_specs=[
            pl.BlockSpec((cols // owned, chunk, rows), lambda i: (i, 0, 0)),
            tok,
            tok,
            tok,
            pl.BlockSpec((3 * HALO, cols), lambda i: (0, i)),
        ],
        out_shape=[
            pltpu.HBM((n_ctx, chunk, rows), bf16),
            jax.ShapeDtypeStruct((rows, width), f32),
            jax.ShapeDtypeStruct((rows, width), f32),
            jax.ShapeDtypeStruct((rows, width), f32),
            jax.ShapeDtypeStruct((3 * HALO, width), f32),
        ],
        scratch_shapes=[
            pltpu.VMEM((3 * HALO, width), f32),
            pltpu.VMEM((3, rows + HALO, cols), f32),
            pltpu.VMEM((rows, cols), bf16),
            pltpu.VMEM((rows, cols), bf16),
        ],
        compiler_params=pltpu.CompilerParams(vmem_limit_bytes=VMEM_LIMIT),
        name="featurize",
    )(*in_hbm(query, key, value, grad), before, short_taps, filt)


WIDE = 2048
BATCH = 4


def shift_right(value, steps):
    return value if steps == 0 else pltpu.roll(value, steps, axis=1)


def shift_left(value, steps):
    return value if steps == 0 else pltpu.roll(value, value.shape[1] - steps, axis=1)


def build_toeplitz(fpad, which, length, v8, toe):
    for lo in range(0, length, WIDE):
        wide = jnp.broadcast_to(fpad[pl.ds(which, 1), lo + LANES : lo + 2 * LANES + WIDE], (8, WIDE + LANES))
        row = lax.broadcasted_iota(jnp.int32, wide.shape, 0)
        for bit in (1, 2, 4):
            wide = jnp.where((row & bit) != 0, shift_right(wide, bit), wide)
        v8[:, lo + LANES : lo + LANES + WIDE] = wide[:, LANES:]
    v8[:, :LANES] = jnp.zeros((8, LANES), f32)
    toe[:, :LANES] = jnp.zeros((LANES, LANES), bf16)

    for lo in range(0, length, WIDE):
        wide = v8[:, lo : lo + LANES + WIDE]
        for p in range(0, LANES // 8, 2):
            pair = [shift_right(wide, 8 * (p + i))[:, LANES:] for i in range(2)]
            toe[8 * p : 8 * p + 16, lo + LANES : lo + LANES + WIDE] = jnp.concatenate(pair, axis=0).astype(bf16)


def fill_filter(x_ref, fpad):
    blocks, chunk, size = x_ref.shape
    fpad[:, : 2 * LANES] = jnp.zeros((SPARE, 2 * LANES), f32)
    for j in range(blocks):
        lo = 2 * LANES + size * j
        fpad[:, lo : lo + size] = x_ref[j, chunk - SPARE :, :].astype(f32)


def toeplitz_rows(toe, k, width):
    base = 2 * k * LANES
    return jnp.concatenate([toe[:, base + LANES : base + LANES + width], toe[:, base : base + width]], axis=0)


def forward_kernel(x_any, y_hbm, fpad, v8, toe, gpad, acc, y_ref, x_ref, sems, *, scale):
    g = pl.program_id(0)
    blocks, chunk, size = x_ref.shape
    rows = blocks * GROUP
    top = BATCH * GROUP

    @pl.when(g == 0)
    def _():
        half = (chunk - SPARE) // 2
        parts = (pl.ds(2 * half, SPARE), pl.ds(0, half))
        copies = [
            pltpu.make_async_copy(x_any.at[:, part, :], x_ref.at[:, part, :], sems.at[i])
            for i, part in enumerate(parts)
        ]
        for copy in copies:
            copy.start()
        copies[0].wait()
        fill_filter(x_ref, fpad)
        copies[1].wait()

    build_toeplitz(fpad, g, blocks * size, v8, toe)
    lines = pl.ds(pl.multiple_of(g * GROUP, GROUP), GROUP)
    gpad[:top, :] = jnp.zeros((top, size), bf16)
    gpad[top:, :] = x_ref[:, lines, :].reshape(rows, size)
    left = jnp.concatenate([gpad[top - GROUP * i : top - GROUP * i + rows, :] for i in range(BATCH)], axis=1)
    for kb in range(blocks // BATCH):
        first = top * kb
        right = jnp.concatenate([toeplitz_rows(toe, BATCH * kb + i, size) for i in range(BATCH)], axis=0)
        part = jnp.dot(left[: rows - first], right, preferred_element_type=f32)
        acc[first:, :] = part if kb == 0 else acc[first:, :] + part
    y_ref[:, lines, :] = (acc[...] * scale).astype(bf16).reshape(blocks, GROUP, size)
    out = pltpu.make_async_copy(y_ref.at[:, lines, :], y_hbm.at[:, lines, :], sems.at[2])
    out.start()
    out.wait()


def backward_kernel(x_any, y_hbm, fpad, v8, toe, gpad, zpad, acc, corr, fgrad, y_ref, x_ref, sems, *, scale):
    g = pl.program_id(0)
    blocks, chunk, size = x_ref.shape
    half = (chunk - SPARE) // 2
    length = blocks * size
    rows = blocks * GROUP
    near = rows // 2
    top = BATCH * GROUP

    @pl.when(g == 0)
    def _():
        x_in = pltpu.make_async_copy(x_any, x_ref, sems.at[2])
        x_in.start()
        x_in.wait()
        fill_filter(x_ref, fpad)
        fgrad[...] = jnp.zeros_like(fgrad)

    build_toeplitz(fpad, g, length, v8, toe)
    lines = pl.ds(pl.multiple_of(g * GROUP, GROUP), GROUP)
    back_lines = pl.ds(pl.multiple_of(half + g * GROUP, GROUP), GROUP)
    gpad[...] = x_ref[:, lines, :].reshape(rows, size)
    zpad[:rows, :] = x_ref[:, back_lines, :].reshape(rows, size)
    zpad[rows:, :] = jnp.zeros((zpad.shape[0] - rows, size), bf16)

    for kb in range(blocks // BATCH):
        first = top * kb
        count = rows - first
        right = toeplitz_rows(toe, BATCH * kb, BATCH * size)
        left = jnp.concatenate(
            [zpad[first + GROUP * i : first + GROUP * i + count, :] for i in range(BATCH)], axis=1
        )
        part = lax.dot_general(left, right, (((1,), (1,)), ((), ())), preferred_element_type=f32)
        acc[:count, :] = part if kb == 0 else acc[:count, :] + part
    y_ref[:, lines, :] = (acc[...] * scale).astype(bf16).reshape(blocks, GROUP, size)
    back_out = pltpu.make_async_copy(y_ref.at[:, lines, :], y_hbm.at[:, lines, :], sems.at[0])
    back_out.start()

    u_t = gpad[...].astype(f32).T.astype(bf16)
    for k in range(blocks):
        depth = rows if k < blocks // 2 else near
        corr[:, size * k : size * (k + 1)] = jnp.dot(
            u_t[:, :depth], zpad[GROUP * k : GROUP * k + depth, :], preferred_element_type=f32
        )
    corr[:, length:] = jnp.zeros((size, corr.shape[1] - length), f32)
    for lo in range(0, length, WIDE):
        total = None
        for p in reversed(range(LANES // 8)):
            part = (
                corr[8 * p : 8 * p + 8, lo : lo + WIDE + LANES]
                + corr[LANES + 8 * p : LANES + 8 * p + 8, lo + LANES : lo + WIDE + 2 * LANES]
            )
            total = part if total is None else shift_left(total, 8) + part
        row = lax.broadcasted_iota(jnp.int32, total.shape, 0)
        for bit in (4, 2, 1):
            total = jnp.where((row & bit) != 0, shift_left(total, bit), total)
        fgrad[pl.ds(g, 1), lo : lo + WIDE] = jnp.sum(total[:, :WIDE], axis=0, keepdims=True) * scale

    @pl.when(g == pl.num_programs(0) - 1)
    def _():
        for j in range(blocks):
            y_ref[j, half:, :] = fgrad[:, size * j : size * (j + 1)].astype(bf16)
        spare = pl.ds(half, SPARE)
        spare_out = pltpu.make_async_copy(y_ref.at[:, spare, :], y_hbm.at[:, spare, :], sems.at[1])
        spare_out.start()
        spare_out.wait()

    back_out.wait()


def longconv(kernel, x, out_rows, scratch, flops, scale, name):
    blocks, chunk, size = x.shape
    length = blocks * size
    shape = (blocks, out_rows, size)
    return pl.pallas_call(
        functools.partial(kernel, scale=scale),
        grid=((chunk - SPARE) // 2 // GROUP,),
        in_specs=[pl.BlockSpec(memory_space=pl.ANY)],
        out_specs=pl.BlockSpec(memory_space=pltpu.HBM),
        out_shape=pltpu.HBM(shape, bf16),
        scratch_shapes=[
            pltpu.VMEM((SPARE, length + 2 * LANES), f32),
            pltpu.VMEM((8, length + LANES), f32),
            pltpu.VMEM((LANES, length + LANES), bf16),
            *scratch,
        ],
        compiler_params=pltpu.CompilerParams(vmem_limit_bytes=VMEM_LIMIT),
        cost_estimate=pl.CostEstimate(flops=flops, bytes_accessed=2_000_000, transcendentals=0),
        name=name,
    )(*in_hbm(x))


def conv_forward(x, scale):
    blocks, chunk, size = x.shape
    half, rows = (chunk - SPARE) // 2, blocks * GROUP
    scratch = [
        pltpu.VMEM((rows + BATCH * GROUP, size), bf16),
        pltpu.VMEM((rows, size), f32),
        pltpu.VMEM((blocks, half, size), bf16),
        pltpu.VMEM(x.shape, bf16),
        pltpu.SemaphoreType.DMA((3,)),
    ]
    return longconv(forward_kernel, x, half, scratch, 2 * rows * rows * size * size // 64, scale, "conv_forward")


def conv_backward(x, scale):
    blocks, chunk, size = x.shape
    half, rows = (chunk - SPARE) // 2, blocks * GROUP
    length = blocks * size
    scratch = [
        pltpu.VMEM((rows, size), bf16),
        pltpu.VMEM((rows + rows // 2, size), bf16),
        pltpu.VMEM((rows, size), f32),
        pltpu.VMEM((size, length + 2 * LANES), f32),
        pltpu.VMEM((SPARE, length), f32),
        pltpu.VMEM((blocks, half + SPARE, size), bf16),
        pltpu.VMEM(x.shape, bf16),
        pltpu.SemaphoreType.DMA((3,)),
    ]
    flops = 4 * rows * rows * size * size // 32
    return longconv(backward_kernel, x, half + SPARE, scratch, flops, scale, "conv_backward")


def tokens(y_ref, count, lanes):
    owners = y_ref.shape[0]
    return y_ref[:, :count, :lanes].reshape(owners * count, lanes).T


def query_grads(conv, qc, kc, vc, grad, skip):
    mixed = conv + skip * (kc * vc).astype(bf16).astype(f32)
    return mixed, grad * mixed


def gate_grads(back, qc, kc, vc, grad, skip):
    grad_gate = back + skip * (grad * qc).astype(bf16).astype(f32)
    return grad_gate * vc, grad_gate * kc


def heads_kernel(y_ref, qc_ref, kc_ref, vc_ref, g_ref, skip_ref, out_ref, *, query):
    half = out_ref.shape[2] // y_ref.shape[0]
    y = tokens(y_ref, half, LANES).astype(f32)[:HALO]
    grad = g_ref[...].astype(f32)[:HALO]
    parts = (query_grads if query else gate_grads)(y, qc_ref[...], kc_ref[...], vc_ref[...], grad, skip_ref[...])
    for which in range(out_ref.shape[0]):
        out_ref[which] = parts[which + query].astype(bf16)


def heads(y, qc, kc, vc, grad, skip, query):
    n_ctx, chunk, rows = y.shape
    width = qc.shape[1]
    count = 1 if query else 2
    cols = 512
    top = pl.BlockSpec((HALO, cols), lambda i: (0, i))
    return pl.pallas_call(
        functools.partial(heads_kernel, query=query),
        grid=(width // cols,),
        in_specs=[
            pl.BlockSpec((cols * n_ctx // width, chunk, LANES), lambda i: (i, 0, 0)),
            top,
            top,
            top,
            pl.BlockSpec((2 * HALO, cols), lambda i: (0, i)),
            pl.BlockSpec((1, cols), lambda i: (0, i)),
        ],
        out_specs=pl.BlockSpec((count, HALO, cols), lambda i: (0, 0, i)),
        out_shape=jax.ShapeDtypeStruct((count, HALO, width), bf16),
        compiler_params=pltpu.CompilerParams(vmem_limit_bytes=VMEM_LIMIT),
        name="query_heads" if query else "gate_heads",
    )(y, qc, kc, vc, *in_hbm(grad), skip)


def spread_kernel(*refs, query):
    if query:
        y_ref, qc_ref, kc_ref, vc_ref, g_ref, skip_ref, taps_ref, after_ref, out_ref, gq_ref, ys, ext = refs
    else:
        y_ref, qc_ref, kc_ref, vc_ref, g_ref, skip_ref, taps_ref, gk_ref, gv_ref, tail_ref, gf_ref, ys, ext = refs
    rows, cols = qc_ref.shape
    owners = y_ref.shape[0]
    half = cols // owners
    count = ext.shape[0]
    ys[...] = tokens(y_ref, half, rows)
    for which in range(count):
        ext[which, rows:, :] = after_ref[0].astype(f32) if query else jnp.zeros((HALO, cols), f32)
    for left in range(0, cols, LANES):
        lanes = slice(left, left + LANES)
        taps = [tap_rows(taps_ref, which, lanes) for which in ((0,) if query else (1, 2))]
        skip = skip_ref[:, lanes]
        for lo in reversed(range(0, rows, CHUNK)):
            part = slice(lo, lo + CHUNK)
            qc = qc_ref[part, lanes]
            args = (ys[part, lanes].astype(f32), qc, kc_ref[part, lanes], vc_ref[part, lanes])
            grad = g_ref[part, lanes].astype(f32)
            if query:
                mixed, gq = query_grads(*args, grad, skip)
                out_ref[part, lanes] = (qc * mixed).astype(bf16)
                signals, targets = (gq,), (gq_ref,)
            else:
                signals, targets = gate_grads(*args, grad, skip), (gk_ref, gv_ref)
            for which in range(count):
                ext[which, part, lanes] = signals[which]
                pieces = [ext[which, lo + j : lo + j + CHUNK, lanes] for j in range(TAPS)]
                targets[which][part, lanes] = weighted(taps[which], pieces).astype(bf16)
    if not query:
        tail_ref[...] = ext[:, rows - TAIL : rows, :]
        owned_groups = gf_ref.shape[0] // owners
        lines = [y_ref[o, half:, :].astype(f32)[:owned_groups] for o in range(owners)]
        gf_ref[...] = jnp.concatenate(lines, axis=0).astype(bf16)


def spread(y, qc, kc, vc, grad, skip, taps_full, after=None):
    query = after is not None
    n_ctx, chunk, rows = y.shape
    width = qc.shape[1]
    cols = COLS
    count = 1 if query else 2
    tok = pl.BlockSpec((rows, cols), lambda i: (0, i))
    in_specs = [
        pl.BlockSpec((cols * n_ctx // width, chunk, rows), lambda i: (i, 0, 0)),
        tok,
        tok,
        tok,
        tok,
        pl.BlockSpec((1, cols), lambda i: (0, i)),
        pl.BlockSpec((3 * HALO, cols), lambda i: (0, i)),
    ]
    out_specs = [tok, tok]
    out_shape = [jax.ShapeDtypeStruct((rows, width), bf16)] * 2
    args = [y, qc, kc, vc, *in_hbm(grad), skip, taps_full]
    if query:
        in_specs.append(pl.BlockSpec((1, HALO, cols), lambda i: (0, 0, i)))
        args.append(after)
    else:
        out_specs += [
            pl.BlockSpec((2, TAIL, cols), lambda i: (0, 0, i)),
            pl.BlockSpec((cols // GROUP, rows), lambda i: (i, 0)),
        ]
        out_shape += [
            jax.ShapeDtypeStruct((2, TAIL, width), f32),
            jax.ShapeDtypeStruct((width // GROUP, rows), bf16),
        ]
    return pl.pallas_call(
        functools.partial(spread_kernel, query=query),
        grid=(width // cols,),
        in_specs=in_specs,
        out_specs=out_specs,
        out_shape=out_shape,
        scratch_shapes=[pltpu.VMEM((rows, cols), bf16), pltpu.VMEM((count, rows + HALO, cols), f32)],
        compiler_params=pltpu.CompilerParams(vmem_limit_bytes=VMEM_LIMIT),
        cost_estimate=pl.CostEstimate(flops=8_000_000, bytes_accessed=6_000_000, transcendentals=0),
        name="query_spread" if query else "gate_spread",
    )(*args)


def tail_kernel(tail_ref, after_ref, taps_ref, gk_in, gv_in, gk_ref, gv_ref, ext):
    ext[:, :TAIL, :] = tail_ref[...]
    ext[:, TAIL:, :] = after_ref[...].astype(f32)
    for which, target in enumerate((gk_ref, gv_ref)):
        for left in range(0, ext.shape[2], LANES):
            lanes = slice(left, left + LANES)
            pieces = [ext[which, j : j + TAIL, lanes] for j in range(TAPS)]
            target[:, lanes] = weighted(tap_rows(taps_ref, which + 1, lanes), pieces).astype(bf16)


def tail(rims, after, taps_full, gk, gv):
    rows, width = gk.shape
    last = rows // TAIL - 1
    strip = pl.BlockSpec((TAIL, width), lambda i: (last, 0))
    anywhere = pl.BlockSpec(memory_space=pl.ANY)
    return pl.pallas_call(
        tail_kernel,
        grid=(1,),
        in_specs=[
            pl.BlockSpec(rims.shape, lambda i: (0, 0, 0)),
            pl.BlockSpec(after.shape, lambda i: (0, 0, 0)),
            pl.BlockSpec(taps_full.shape, lambda i: (0, 0)),
            anywhere,
            anywhere,
        ],
        out_specs=[strip] * 2,
        out_shape=[jax.ShapeDtypeStruct(gk.shape, bf16)] * 2,
        scratch_shapes=[pltpu.VMEM((2, TAIL + HALO, width), f32)],
        input_output_aliases={3: 0, 4: 1},
        compiler_params=pltpu.CompilerParams(vmem_limit_bytes=VMEM_LIMIT),
        name="tail",
    )(rims, after, taps_full, gk, gv)


def body(query_feats, key_feats, value_feats, short_taps, long_filter, skip_gain, out_grad):
    tok_rows, width = query_feats.shape
    n_ctx = lax.axis_size("ctx")
    scale = 1.0 / math.sqrt(tok_rows * n_ctx)
    skip = skip_gain.reshape(1, width)
    before = shifted(last_rows(query_feats, key_feats, value_feats), "ctx", 1)
    x, qc, kc, vc, taps = featurize(
        query_feats, key_feats, value_feats, out_grad, before, short_taps, long_filter.T, n_ctx
    )
    x = lax.all_to_all(x, "ctx", 0, 0, tiled=True)
    conv = lax.all_to_all(conv_forward(x, scale), "ctx", 0, 0, tiled=True)
    back, conv = lax.optimization_barrier((conv_backward(x, scale), conv))
    back = lax.all_to_all(back, "ctx", 0, 0, tiled=True)
    after = shifted(heads(conv, qc, kc, vc, out_grad, skip, True), "ctx", -1)
    mixed_out, gq = spread(conv, qc, kc, vc, out_grad, skip, taps, after)
    back, mixed_out, gq = lax.optimization_barrier((back, mixed_out, gq))
    after = shifted(heads(back, qc, kc, vc, out_grad, skip, False), "ctx", -1)
    gk, gv, rims, gf = spread(back, qc, kc, vc, out_grad, skip, taps)
    gk, gv = tail(rims, after, taps, gk, gv)
    return (mixed_out, gq, gk, gv, gf.T)


def solution(mesh):
    in_specs = (
        P("ctx", "tp"),
        P("ctx", "tp"),
        P("ctx", "tp"),
        P(None, None, "tp"),
        P("ctx", "tp"),
        P("tp"),
        P("ctx", "tp"),
    )
    out_specs = (P("ctx", "tp"),) * 5
    return jax.shard_map(body, mesh=mesh, in_specs=in_specs, out_specs=out_specs, check_vma=False)
```

time: 124 us -> 147 us (1.19)
  the two profiles are of different devices: /device:TPU:38 before, /device:TPU:24 now
where the time goes in v2:
time: 147 us; the launch traced here: 146 us
  starting transfers between devices  52.3 us (36%)
  Pallas kernels  46.8 us (32%)
  blocking collectives  33.8 us (23%)
  waiting for transfers between devices  12.1 us (8%)
    all_to_all x1, blocking collectives, body(): x = lax.all_to_all(x, 'ctx', 0, 0, tiled=True)  33.8 us
    pallas_call x2, Pallas kernels, longconv(): pl.pallas_call(functools.partial(kernel, scale=scale), grid=((chunk - SPA...  28 us
    ppermute x3, starting transfers between devices, shifted(): lax.ppermute(value, axis, [(source, source + steps) for source in range(i...  26.7 us
    all_to_all x1, starting transfers between devices, body(): conv = lax.all_to_all(conv_forward(x, scale), 'ctx', 0, 0, tiled=True)  13.3 us
    all_to_all x1, starting transfers between devices, body(): back = lax.all_to_all(back, 'ctx', 0, 0, tiled=True)  12.3 us
    ppermute x3, waiting for transfers between devices, shifted(): lax.ppermute(value, axis, [(source, source + steps) for source in range(i...  11.6 us
    pallas_call x2, Pallas kernels, spread(): pl.pallas_call(functools.partial(spread_kernel, query=query), grid=(width...  8.95 us
    pallas_call x1, Pallas kernels, featurize(): pl.pallas_call(featurize_kernel, grid=(width // cols,), in_specs=[tok, to...  6.16 us
  transfers between devices with their start and end apart: 5, of which 3 were waited for; matrix products, arithmetic and copies ran while one was open for 0% of the time, Pallas kernels for 20%

profile of v2, /device:TPU:24, one launch (start us, length us, event | category | flops | bytes accessed | tf_op | source)
XLA Modules:
  0.0 145.7 jit_solution(6757134356827518352)
XLA Ops:
  0.6 0.0 copy-start.1
  0.6 0.0 copy-start.2
  0.7 0.8 rims.1
  1.5 3.4 %collective-permute-start = (bf16[3,8,1024]{2,1,0:T(8,128)(2,1)S(1)}, bf16[3,8,1024]{2,1,0:T(8,128)(2,1)S(1)}, u32[]{:S(2)}, u32[]{:S(2)}) collective-permute-start(bf16[3,8,1024]{2,1,0:T(8,128)(2,1)S(1)} %rims.1), channel_id=1, source_target_pairs={{0,8},{8,16},{16,24},{24,32},{32,40},{40,48},{48,56},{56,64},{64,7... | collective-permute-start | bytes 147464 | tf_op jit(solution)/shard_map/ppermute | solution.py:30
  4.9 10.1 %collective-permute-done.before_ref = bf16[3,8,1024]{2,1,0:T(8,128)(2,1)S(1)} collective-permute-done((bf16[3,8,1024]{2,1,0:T(8,128)(2,1)S(1)}, bf16[3,8,1024]{2,1,0:T(8,128)(2,1)S(1)}, u32[]{:S(2)}, u32[]{:S(2)}) %collective-permute-start) | collective-permute-done | bytes 49184 | tf_op jit(solution)/shard_map/ppermute | solution.py:30
  15.0 0.0 copy-done.1
  15.0 0.0 copy-done.2
  15.0 6.2 %featurize.1 = (bf16[32,72,256]{2,1,0:T(8,128)(2,1)}, f32[256,1024]{1,0:T(8,128)S(1)}, f32[256,1024]{1,0:T(8,128)S(1)}, f32[256,1024]{1,0:T(8,128)S(1)}, f32[24,1024]{1,0:T(8,128)S(1)}) custom-call(bf16[256,1024]{1,0:T(8,128)(2,1)} %q_ref.3, bf16[256,1024]{1,0:T(8,128)(2,1)} %k_ref.3, bf16[256,1024]{1,0:T(8,128)(2,1)} %v_ref.3, bf16[256,1024]{1,0:T(8,128)(2,1)} %g_ref.5, ...), custom_call_target="tpu_custom_call" | custom-call | tf_op jit(solution)/shard_map/featurize/pallas_call | solution.py:128
  21.1 33.8 %all_to_all.15.x_any = bf16[32,72,256]{2,1,0:T(8,128)(2,1)} all-to-all(bf16[32,72,256]{2,1,0:T(8,128)(2,1)} %get-tuple-element.23), channel_id=1, replica_groups=mesh['ctx'=32,'tp'=8] {'ctx'}, dimensions={0} | all-to-all | bytes 2359296 | tf_op jit(solution)/shard_map/all_to_all | solution.py:538
  54.9 8.5 %conv_forward.1 = bf16[32,32,256]{2,1,0:T(8,128)(2,1)} custom-call(bf16[32,72,256]{2,1,0:T(8,128)(2,1)} %all_to_all.15.x_any), custom_call_target="tpu_custom_call" | custom-call | flops 536870912 | bytes 2000000 | tf_op jit(solution)/shard_map/conv_forward/pallas_call | solution.py:316
  63.4 13.3 %all-to-all-start.1 = ((bf16[32,32,256]{2,1,0:T(8,128)(2,1)}), bf16[32,32,256]{2,1,0:T(8,128)(2,1)}, u32[]{:S(2)}, u32[]{:S(2)}) async-start(bf16[32,32,256]{2,1,0:T(8,128)(2,1)} %conv_forward.1), calls=%async_computation.1 | async-start | bytes 1048576 | tf_op jit(solution)/shard_map/all_to_all | solution.py:539
  76.8 19.5 %conv_backward.1 = bf16[32,40,256]{2,1,0:T(8,128)(2,1)} custom-call(bf16[32,72,256]{2,1,0:T(8,128)(2,1)} %all_to_all.15.x_any), custom_call_target="tpu_custom_call" | custom-call | flops 2147483648 | bytes 2000000 | tf_op jit(solution)/shard_map/conv_backward/pallas_call | solution.py:316
  96.2 0.0 copy-start
  96.3 0.0 all-to-all-done.1.y_ref.refs_0_
  96.3 12.3 %all-to-all-start.2 = ((bf16[32,40,256]{2,1,0:T(8,128)(2,1)}), bf16[32,40,256]{2,1,0:T(8,128)(2,1)}, u32[]{:S(2)}, u32[]{:S(2)}) async-start(bf16[32,40,256]{2,1,0:T(8,128)(2,1)} %conv_backward.1), calls=%async_computation.2 | async-start | bytes 1310720 | tf_op jit(solution)/shard_map/all_to_all | solution.py:541
  108.5 0.0 copy-done
  108.5 1.1 query_heads.1
  109.6 9.7 %collective-permute-start.1 = (bf16[1,8,1024]{2,1,0:T(8,128)(2,1)S(1)}, bf16[1,8,1024]{2,1,0:T(8,128)(2,1)S(1)}, u32[]{:S(2)}, u32[]{:S(2)}) collective-permute-start(bf16[1,8,1024]{2,1,0:T(8,128)(2,1)S(1)} %query_heads.1), channel_id=1, source_target_pairs={{8,0},{16,8},{24,16},{32,24},{40,32},{48,40},{56,48},{64,56},{72,6... | collective-permute-start | bytes 49160 | tf_op jit(solution)/shard_map/ppermute | solution.py:30
  119.3 1.4 collective-permute-done.1.refs_7_
  120.7 4.2 %query_spread.1 = (bf16[256,1024]{1,0:T(8,128)(2,1)}, bf16[256,1024]{1,0:T(8,128)(2,1)}) custom-call(bf16[32,32,256]{2,1,0:T(8,128)(2,1)} %all-to-all-done.1.y_ref.refs_0_, f32[256,1024]{1,0:T(8,128)S(1)} %get-tuple-element.26.qc_ref.refs_1_, f32[256,1024]{1,0:T(8,128)S(1)} %get-tuple-element.27.kc_ref.refs_2_, ...), custom_call_target="tpu_custom_call" | custom-call | flops 8000000 | bytes 6000000 | tf_op jit(solution)/shard_map/query_spread/pallas_call | solution.py:482
  124.9 0.6 all-to-all-done.2.refs_0_.y_ref
  125.5 1.1 gate_heads.1
  126.6 13.7 %collective-permute-start.2 = (bf16[2,8,1024]{2,1,0:T(8,128)(2,1)S(1)}, bf16[2,8,1024]{2,1,0:T(8,128)(2,1)S(1)}, u32[]{:S(2)}, u32[]{:S(2)}) collective-permute-start(bf16[2,8,1024]{2,1,0:T(8,128)(2,1)S(1)} %gate_heads.1), channel_id=1, source_target_pairs={{8,0},{16,8},{24,16},{32,24},{40,32},{48,40},{56,48},{64,56},{72,6... | collective-permute-start | bytes 98312 | tf_op jit(solution)/shard_map/ppermute | solution.py:30
  140.2 4.7 %gate_spread.1 = (bf16[256,1024]{1,0:T(8,128)(2,1)}, bf16[256,1024]{1,0:T(8,128)(2,1)}, f32[2,16,1024]{2,1,0:T(8,128)S(1)}, bf16[64,256]{1,0:T(8,128)(2,1)}) custom-call(bf16[32,40,256]{2,1,0:T(8,128)(2,1)} %all-to-all-done.2.refs_0_.y_ref, f32[256,1024]{1,0:T(8,128)S(1)} %get-tuple-element.26.qc_ref.refs_1_, ...), custom_call_target="tpu_custom_call" | custom-call | flops 8000000 | bytes 6000000 | tf_op jit(solution)/shard_map/gate_spread/pallas_call | solution.py:482
  145.0 0.0 collective-permute-done.2.after_ref
  145.0 0.8 tail.1
Async XLA Ops:
  0.6 14.4 %copy-start.1 = (bf16[256,64]{0,1:T(8,128)(2,1)S(1)}, bf16[256,64]{0,1:T(8,128)(2,1)}, u32[]{:S(2)}) copy-start(bf16[256,64]{0,1:T(8,128)(2,1)} %param.11) | copy-start | bytes 98308
  0.6 14.3 %copy-start.2 = (f32[3,7,64]{2,1,0:T(8,128)S(1)}, f32[3,7,64]{2,1,0:T(8,128)}, u32[]{:S(2)}) copy-start(f32[3,7,64]{2,1,0:T(8,128)} %taps_ref.1) | copy-start | bytes 16132
  1.5 13.5 %collective-permute-start = (bf16[3,8,1024]{2,1,0:T(8,128)(2,1)S(1)}, bf16[3,8,1024]{2,1,0:T(8,128)(2,1)S(1)}, u32[]{:S(2)}, u32[]{:S(2)}) collective-permute-start(bf16[3,8,1024]{2,1,0:T(8,128)(2,1)S(1)} %rims.1), channel_id=1, source_target_pairs={{0,8},{8,16},{16,24},{24,32},{32,40},{40,48},{48,56},{56,64},{64,7... | collective-permute-start | bytes 147464 | tf_op jit(solution)/shard_map/ppermute | solution.py:30
  63.4 32.8 %all-to-all-start.1 = ((bf16[32,32,256]{2,1,0:T(8,128)(2,1)}), bf16[32,32,256]{2,1,0:T(8,128)(2,1)}, u32[]{:S(2)}, u32[]{:S(2)}) async-start(bf16[32,32,256]{2,1,0:T(8,128)(2,1)} %conv_forward.1), calls=%async_computation.1 | async-start | bytes 1048576 | tf_op jit(solution)/shard_map/all_to_all | solution.py:539
  96.2 12.3 %copy-start = (f32[1024]{0:T(1024)S(1)}, f32[1024]{0:T(1024)}, u32[]{:S(2)}) copy-start(f32[1024]{0:T(1024)} %param.12) | copy-start | bytes 12292
  96.3 29.2 %all-to-all-start.2 = ((bf16[32,40,256]{2,1,0:T(8,128)(2,1)}), bf16[32,40,256]{2,1,0:T(8,128)(2,1)}, u32[]{:S(2)}, u32[]{:S(2)}) async-start(bf16[32,40,256]{2,1,0:T(8,128)(2,1)} %conv_backward.1), calls=%async_computation.2 | async-start | bytes 1310720 | tf_op jit(solution)/shard_map/all_to_all | solution.py:541
  109.6 11.1 %collective-permute-start.1 = (bf16[1,8,1024]{2,1,0:T(8,128)(2,1)S(1)}, bf16[1,8,1024]{2,1,0:T(8,128)(2,1)S(1)}, u32[]{:S(2)}, u32[]{:S(2)}) collective-permute-start(bf16[1,8,1024]{2,1,0:T(8,128)(2,1)S(1)} %query_heads.1), channel_id=1, source_target_pairs={{8,0},{16,8},{24,16},{32,24},{40,32},{48,40},{56,48},{64,56},{72,6... | collective-permute-start | bytes 49160 | tf_op jit(solution)/shard_map/ppermute | solution.py:30
  126.6 18.4 %collective-permute-start.2 = (bf16[2,8,1024]{2,1,0:T(8,128)(2,1)S(1)}, bf16[2,8,1024]{2,1,0:T(8,128)(2,1)S(1)}, u32[]{:S(2)}, u32[]{:S(2)}) collective-permute-start(bf16[2,8,1024]{2,1,0:T(8,128)(2,1)S(1)} %gate_heads.1), channel_id=1, source_target_pairs={{8,0},{16,8},{24,16},{32,24},{40,32},{48,40},{56,48},{64,56},{72,6... | collective-permute-start | bytes 98312 | tf_op jit(solution)/shard_map/ppermute | solution.py:30

commit v3 on v1

v3 whole, which is shorter than its diff:
```python
import functools
import math

import jax
import jax.numpy as jnp
from jax import lax
from jax.experimental import pallas as pl
from jax.experimental.pallas import tpu as pltpu
from jax.sharding import PartitionSpec as P

D = 8192
SHORT_GROUPS = 512
GROUP = D // SHORT_GROUPS
TAPS = 7
HALO = 8
TAIL = 16
COLS = 256
CHUNK = 64
SPARE = 8
LANES = 128
VMEM_LIMIT = 30 * 1024 * 1024

f32 = jnp.float32
bf16 = jnp.bfloat16


def shifted(value, axis, steps):
    count = lax.axis_size(axis)
    initial, last = (max(0, -steps), min(count, count - steps))
    return lax.ppermute(value, axis, [(source, source + steps) for source in range(initial, last)])


def rims_kernel(q_ref, k_ref, v_ref, out_ref):
    for which, ref in enumerate((q_ref, k_ref, v_ref)):
        out_ref[which] = ref[...].astype(f32)[HALO:].astype(bf16)


def last_rows(query, key, value):
    rows, width = query.shape
    last = rows // TAIL - 1
    strip = pl.BlockSpec((TAIL, width), lambda i: (last, 0))
    return pl.pallas_call(
        rims_kernel,
        grid=(1,),
        in_specs=[strip] * 3,
        out_specs=pl.BlockSpec((3, HALO, width), lambda i: (0, 0, 0)),
        out_shape=jax.ShapeDtypeStruct((3, HALO, width), bf16),
        compiler_params=pltpu.CompilerParams(vmem_limit_bytes=VMEM_LIMIT),
        name="rims",
    )(*in_hbm(query, key, value))


def widen(short_taps):
    count, _, groups = short_taps.shape
    padded = jnp.pad(short_taps, ((0, 0), (0, HALO - TAPS), (0, 0)))
    return jnp.repeat(padded, GROUP, axis=2).reshape(count * HALO, groups * GROUP)


def tap_rows(taps_ref, which, lanes):
    return [
        jnp.broadcast_to(taps_ref[HALO * which + j : HALO * which + j + 1, lanes], (8, LANES)) for j in range(TAPS)
    ]


def weighted(taps, pieces):
    total = None
    for tap, piece in zip(taps, pieces):
        term = piece.reshape(piece.shape[0] // 8, 8, LANES) * tap[None]
        total = term if total is None else total + term
    return total.reshape(-1, LANES)


def featurize_kernel(
    q_ref, k_ref, v_ref, g_ref, before_ref, taps_ref, f_ref, x_ref, qc_ref, kc_ref, vc_ref, ext, gated, mix
):
    rows, cols = q_ref.shape
    owners = x_ref.shape[0]
    half = cols // owners
    owned_groups = half // GROUP
    start = pl.program_id(0) * cols
    here = pl.ds(pl.multiple_of(start, cols), cols)
    for which, ref in enumerate((q_ref, k_ref, v_ref)):
        ext[which, :HALO, :] = before_ref[which, :, here].astype(f32)
        ext[which, HALO:, :] = ref[...].astype(f32)
    for left in range(0, cols, LANES):
        lanes = slice(left, left + LANES)
        there = pl.ds(pl.multiple_of(start + left, LANES), LANES)
        taps = [tap_rows(taps_ref, which, there) for which in range(3)]
        for lo in range(0, rows, CHUNK):
            part = slice(lo, lo + CHUNK)

            def conv(which):
                first = HALO + lo
                return weighted(taps[which], [ext[which, first - j : first - j + CHUNK, lanes] for j in range(TAPS)])

            key_conv = conv(1)
            kc_ref[part, there] = key_conv
            value_conv = conv(2)
            vc_ref[part, there] = value_conv
            gated[part, lanes] = (key_conv * value_conv).astype(bf16)
            query_conv = conv(0)
            qc_ref[part, there] = query_conv
            mix[part, lanes] = (g_ref[part, lanes].astype(f32) * query_conv).astype(bf16)
    x_ref[:, :half, :] = gated[...].T.reshape(owners, half, rows)
    x_ref[:, half : 2 * half, :] = mix[...].T.reshape(owners, half, rows)
    lines = owners * owned_groups
    filt = f_ref[pl.ds(pl.multiple_of(pl.program_id(0) * lines, lines), lines), :].astype(f32)
    blank = jnp.zeros((SPARE - owned_groups, rows), f32)
    for owner in range(owners):
        mine = filt[owner * owned_groups : (owner + 1) * owned_groups]
        x_ref[owner, 2 * half :, :] = jnp.concatenate([mine, blank], axis=0).astype(bf16)


def in_hbm(*arrays):
    return [pltpu.with_memory_space_constraint(a, pltpu.HBM) for a in arrays]


def featurize(query, key, value, grad, before, taps_full, filt, n_ctx):
    rows, width = query.shape
    owned = width // n_ctx
    chunk = 2 * owned + SPARE
    cols = COLS
    tok = pl.BlockSpec((rows, cols), lambda i: (0, i))
    resident = pl.BlockSpec(memory_space=pltpu.VMEM)
    return pl.pallas_call(
        featurize_kernel,
        grid=(width // cols,),
        in_specs=[
            tok,
            tok,
            tok,
            tok,
            resident,
            resident,
            resident,
        ],
        out_specs=[
            pl.BlockSpec((cols // owned, chunk, rows), lambda i: (i, 0, 0)),
            resident,
            resident,
            resident,
        ],
        out_shape=[
            pltpu.HBM((n_ctx, chunk, rows), bf16),
            jax.ShapeDtypeStruct((rows, width), f32),
            jax.ShapeDtypeStruct((rows, width), f32),
            jax.ShapeDtypeStruct((rows, width), f32),
        ],
        scratch_shapes=[
            pltpu.VMEM((3, rows + HALO, cols), f32),
            pltpu.VMEM((rows, cols), bf16),
            pltpu.VMEM((rows, cols), bf16),
        ],
        compiler_params=pltpu.CompilerParams(vmem_limit_bytes=VMEM_LIMIT),
        name="featurize",
    )(*in_hbm(query, key, value, grad), before, taps_full, filt)


WIDE = 2048


def shift_left(value, steps):
    return value if steps == 0 else pltpu.roll(value, value.shape[1] - steps, axis=1)


def build_toeplitz(fpad, which, length, toe):
    toe[:, :LANES] = jnp.zeros((LANES, LANES), bf16)
    for lo in range(0, length, WIDE // 2):
        for p in range(0, LANES, 16):
            lanes = slice(lo + LANES, lo + 2 * LANES + WIDE // 2)
            wide = jnp.broadcast_to(fpad[pl.ds(which, 1), lanes], (16, WIDE // 2 + LANES))
            wide = pltpu.roll(wide, p, axis=1, stride=1, stride_axis=0)
            toe[p : p + 16, lo + LANES : lo + LANES + WIDE // 2] = wide[:, LANES:].astype(bf16)


def longconv_kernel(x_ref, y_hbm, fpad, toe, gpad, zpad, acc, corr, fgrad, y_ref, sems, *, scale):
    g = pl.program_id(0)
    blocks, chunk, size = x_ref.shape
    half = (chunk - SPARE) // 2
    length = blocks * size
    rows = blocks * GROUP
    group = GROUP
    groups = half // group
    batch = 2
    top = batch * group

    @pl.when(g == 0)
    def _():
        fpad[:, : 2 * LANES] = jnp.zeros((SPARE, 2 * LANES), f32)
        for j in range(blocks):
            lo = 2 * LANES + size * j
            fpad[:, lo : lo + size] = x_ref[j, 2 * half :, :].astype(f32)
        fgrad[...] = jnp.zeros_like(fgrad)

    build_toeplitz(fpad, g, length, toe)
    gpad[:top, :] = jnp.zeros((top, size), bf16)
    lines = pl.ds(pl.multiple_of(g * group, group), group)
    back_lines = pl.ds(pl.multiple_of(half + g * group, group), group)
    gpad[top:, :] = x_ref[:, lines, :].reshape(rows, size)
    zpad[:rows, :] = x_ref[:, back_lines, :].reshape(rows, size)
    zpad[rows:, :] = jnp.zeros((zpad.shape[0] - rows, size), bf16)

    u_t = gpad[top:, :].astype(f32).T.astype(bf16)
    near = rows // 2
    for k in range(blocks):
        depth = rows if k < blocks // 2 else near
        corr[:, size * k : size * (k + 1)] = jnp.dot(
            u_t[:, :depth], zpad[group * k : group * k + depth, :], preferred_element_type=f32
        )
    corr[:, length:] = jnp.zeros((size, corr.shape[1] - length), f32)
    for lo in range(0, length, WIDE):
        total = None
        for p in reversed(range(LANES // 8)):
            part = (
                corr[8 * p : 8 * p + 8, lo : lo + WIDE + LANES]
                + corr[LANES + 8 * p : LANES + 8 * p + 8, lo + LANES : lo + WIDE + 2 * LANES]
            )
            total = part if total is None else shift_left(total, 8) + part
        row = lax.broadcasted_iota(jnp.int32, total.shape, 0)
        for bit in (4, 2, 1):
            total = jnp.where((row & bit) != 0, shift_left(total, bit), total)
        fgrad[pl.ds(g, 1), lo : lo + WIDE] = jnp.sum(total[:, :WIDE], axis=0, keepdims=True) * scale

    def toeplitz_rows(k, width):
        base = 2 * k * LANES
        return jnp.concatenate(
            [toe[:, base + LANES : base + LANES + width], toe[:, base : base + width]], axis=0
        )

    left = jnp.concatenate([gpad[top - group * i : top - group * i + rows, :] for i in range(batch)], axis=1)
    for kb in range(blocks // batch):
        first = top * kb
        right = jnp.concatenate([toeplitz_rows(batch * kb + i, size) for i in range(batch)], axis=0)
        part = jnp.dot(left[: rows - first], right, preferred_element_type=f32)
        acc[first:, :] = part if kb == 0 else acc[first:, :] + part
    y_ref[:, lines, :] = (acc[...] * scale).astype(bf16).reshape(blocks, group, size)
    conv_out = pltpu.make_async_copy(y_ref.at[:, lines, :], y_hbm.at[:, lines, :], sems.at[g, 0])
    conv_out.start()

    for kb in range(blocks // batch):
        first = top * kb
        right = toeplitz_rows(batch * kb, batch * size)
        count = rows - first
        left = jnp.concatenate(
            [zpad[first + group * i : first + group * i + count, :] for i in range(batch)], axis=1
        )
        part = lax.dot_general(left, right, (((1,), (1,)), ((), ())), preferred_element_type=f32)
        acc[:count, :] = part if kb == 0 else acc[:count, :] + part
    y_ref[:, back_lines, :] = (acc[...] * scale).astype(bf16).reshape(blocks, group, size)
    back_out = pltpu.make_async_copy(y_ref.at[:, back_lines, :], y_hbm.at[:, back_lines, :], sems.at[g, 1])
    back_out.start()

    @pl.when(g == groups - 1)
    def _():
        for j in range(blocks):
            y_ref[j, 2 * half :, :] = fgrad[:, size * j : size * (j + 1)].astype(bf16)
        spare = pl.ds(2 * half, SPARE)
        spare_out = pltpu.make_async_copy(y_ref.at[:, spare, :], y_hbm.at[:, spare, :], sems.at[0, 2])
        spare_out.start()
        for i in range(groups):
            for k, first in enumerate((0, half)):
                part = pl.ds(first + i * group, group)
                pltpu.make_async_copy(y_ref.at[:, part, :], y_hbm.at[:, part, :], sems.at[i, k]).wait()
        spare_out.wait()


def longconv(x, scale):
    blocks, chunk, size = x.shape
    length = blocks * size
    rows = blocks * GROUP
    groups = (chunk - SPARE) // 2 // GROUP
    return pl.pallas_call(
        functools.partial(longconv_kernel, scale=scale),
        grid=(groups,),
        in_specs=[pl.BlockSpec(memory_space=pltpu.VMEM)],
        out_specs=pl.BlockSpec(memory_space=pltpu.HBM),
        out_shape=pltpu.HBM(x.shape, bf16),
        scratch_shapes=[
            pltpu.VMEM((SPARE, length + 2 * LANES), f32),
            pltpu.VMEM((LANES, length + LANES), bf16),
            pltpu.VMEM((rows + 2 * GROUP, size), bf16),
            pltpu.VMEM((rows + rows // 2, size), bf16),
            pltpu.VMEM((rows, size), f32),
            pltpu.VMEM((size, length + 2 * LANES), f32),
            pltpu.VMEM((SPARE, length), f32),
            pltpu.VMEM(x.shape, bf16),
            pltpu.SemaphoreType.DMA((groups, 3)),
        ],
        compiler_params=pltpu.CompilerParams(vmem_limit_bytes=VMEM_LIMIT),
        name="longconv",
    )(x)


def tokens(y_ref, lo, count, lanes):
    owners = y_ref.shape[0]
    return y_ref[:, lo : lo + count, :lanes].reshape(owners * count, lanes).T


def grads(conv, back, qc, kc, vc, grad, skip):
    gated = (kc * vc).astype(bf16).astype(f32)
    grad_mix = (grad * qc).astype(bf16).astype(f32)
    mixed = conv + skip * gated
    grad_gate = back + skip * grad_mix
    return mixed, grad * mixed, grad_gate * vc, grad_gate * kc


def heads_kernel(y_ref, qc_ref, kc_ref, vc_ref, g_ref, skip_ref, out_ref):
    half = (y_ref.shape[1] - SPARE) // 2
    conv = tokens(y_ref, 0, half, LANES).astype(f32)[:HALO]
    back = tokens(y_ref, half, half, LANES).astype(f32)[:HALO]
    grad = g_ref[...].astype(f32)[:HALO]
    _, gq, gk, gv = grads(conv, back, qc_ref[...], kc_ref[...], vc_ref[...], grad, skip_ref[...])
    out_ref[0] = gq.astype(bf16)
    out_ref[1] = gk.astype(bf16)
    out_ref[2] = gv.astype(bf16)


def heads(y, qc, kc, vc, grad, skip):
    n_ctx, chunk, rows = y.shape
    width = qc.shape[1]
    cols = 512
    top = pl.BlockSpec((HALO, cols), lambda i: (0, i))
    return pl.pallas_call(
        heads_kernel,
        grid=(width // cols,),
        in_specs=[
            pl.BlockSpec((cols * n_ctx // width, chunk, LANES), lambda i: (i, 0, 0)),
            top,
            top,
            top,
            pl.BlockSpec((2 * HALO, cols), lambda i: (0, i)),
            pl.BlockSpec((1, cols), lambda i: (0, i)),
        ],
        out_specs=pl.BlockSpec((3, HALO, cols), lambda i: (0, 0, i)),
        out_shape=jax.ShapeDtypeStruct((3, HALO, width), bf16),
        compiler_params=pltpu.CompilerParams(vmem_limit_bytes=VMEM_LIMIT),
        name="heads",
    )(y, qc, kc, vc, *in_hbm(grad), skip)


def spread_kernel(
    y_ref, qc_ref, kc_ref, vc_ref, g_ref, skip_ref, taps_ref, out_ref, gq_ref, gk_ref, gv_ref, tail_ref, gf_ref, conv, back, ext
):
    rows, cols = g_ref.shape
    half = (y_ref.shape[1] - SPARE) // 2
    owners = cols // half
    owned_groups = gf_ref.shape[0] // owners
    step = pl.program_id(0)
    y_ref = y_ref.at[pl.ds(step * owners, owners)]
    lines = [y_ref[o, 2 * half :, :].astype(f32)[:owned_groups] for o in range(owners)]
    gf_ref[...] = jnp.concatenate(lines, axis=0).astype(bf16)
    conv[...] = tokens(y_ref, 0, half, rows)
    back[...] = tokens(y_ref, half, half, rows)
    for which in range(3):
        ext[which, rows:, :] = jnp.zeros((HALO, cols), f32)
    for left in range(0, cols, LANES):
        lanes = slice(left, left + LANES)
        there = pl.ds(pl.multiple_of(step * cols + left, LANES), LANES)
        taps = [tap_rows(taps_ref, which, there) for which in range(3)]
        for lo in reversed(range(0, rows, CHUNK)):
            part = slice(lo, lo + CHUNK)
            qc = qc_ref[part, there]
            mixed, *signals = grads(
                conv[part, lanes].astype(f32),
                back[part, lanes].astype(f32),
                qc,
                kc_ref[part, there],
                vc_ref[part, there],
                g_ref[part, lanes].astype(f32),
                skip_ref[:, there],
            )
            out_ref[part, lanes] = (qc * mixed).astype(bf16)
            for which, target in enumerate((gq_ref, gk_ref, gv_ref)):
                ext[which, part, lanes] = signals[which]
                pieces = [ext[which, lo + j : lo + j + CHUNK, lanes] for j in range(TAPS)]
                target[part, lanes] = weighted(taps[which], pieces).astype(bf16)
    tail_ref[...] = ext[:, rows - TAIL : rows, :]


def spread(y, qc, kc, vc, grad, skip, taps_full):
    n_ctx, chunk, rows = y.shape
    width = qc.shape[1]
    cols = COLS
    tok = pl.BlockSpec((rows, cols), lambda i: (0, i))
    resident = pl.BlockSpec(memory_space=pltpu.VMEM)
    return pl.pallas_call(
        spread_kernel,
        grid=(width // cols,),
        in_specs=[resident] * 4 + [tok] + [resident] * 2,
        out_specs=[tok] * 4
        + [
            pl.BlockSpec((3, TAIL, cols), lambda i: (0, 0, i)),
            pl.BlockSpec((cols // GROUP, rows), lambda i: (i, 0)),
        ],
        out_shape=[jax.ShapeDtypeStruct((rows, width), bf16)] * 4
        + [jax.ShapeDtypeStruct((3, TAIL, width), f32), jax.ShapeDtypeStruct((width // GROUP, rows), bf16)],
        scratch_shapes=[
            pltpu.VMEM((rows, cols), bf16),
            pltpu.VMEM((rows, cols), bf16),
            pltpu.VMEM((3, rows + HALO, cols), f32),
        ],
        compiler_params=pltpu.CompilerParams(vmem_limit_bytes=VMEM_LIMIT),
        cost_estimate=pl.CostEstimate(flops=12_000_000, bytes_accessed=8_000_000, transcendentals=0),
        name="spread",
    )(y, qc, kc, vc, *in_hbm(grad), skip, taps_full)


def tail_kernel(tail_ref, after_ref, taps_ref, gq_in, gk_in, gv_in, gq_ref, gk_ref, gv_ref, ext):
    ext[:, :TAIL, :] = tail_ref[...]
    ext[:, TAIL:, :] = after_ref[...].astype(f32)
    for which, target in enumerate((gq_ref, gk_ref, gv_ref)):
        for left in range(0, ext.shape[2], LANES):
            lanes = slice(left, left + LANES)
            pieces = [ext[which, j : j + TAIL, lanes] for j in range(TAPS)]
            target[:, lanes] = weighted(tap_rows(taps_ref, which, lanes), pieces).astype(bf16)


def tail(rims, after, taps_full, gq, gk, gv):
    rows, width = gq.shape
    last = rows // TAIL - 1
    strip = pl.BlockSpec((TAIL, width), lambda i: (last, 0))
    anywhere = pl.BlockSpec(memory_space=pl.ANY)
    return pl.pallas_call(
        tail_kernel,
        grid=(1,),
        in_specs=[
            pl.BlockSpec(rims.shape, lambda i: (0, 0, 0)),
            pl.BlockSpec(after.shape, lambda i: (0, 0, 0)),
            pl.BlockSpec(taps_full.shape, lambda i: (0, 0)),
            anywhere,
            anywhere,
            anywhere,
        ],
        out_specs=[strip] * 3,
        out_shape=[jax.ShapeDtypeStruct(gq.shape, bf16)] * 3,
        scratch_shapes=[pltpu.VMEM((3, TAIL + HALO, width), f32)],
        input_output_aliases={3: 0, 4: 1, 5: 2},
        compiler_params=pltpu.CompilerParams(vmem_limit_bytes=VMEM_LIMIT),
        name="tail",
    )(rims, after, taps_full, gq, gk, gv)


def body(query_feats, key_feats, value_feats, short_taps, long_filter, skip_gain, out_grad):
    tok_rows, width = query_feats.shape
    n_ctx = lax.axis_size("ctx")
    length = tok_rows * n_ctx
    taps_full = widen(short_taps)
    skip = skip_gain.reshape(1, width)
    before = shifted(last_rows(query_feats, key_feats, value_feats), "ctx", 1)
    x, qc, kc, vc = featurize(query_feats, key_feats, value_feats, out_grad, before, taps_full, long_filter.T, n_ctx)
    x = lax.all_to_all(x, "ctx", 0, 0, tiled=True)
    y = longconv(x, 1.0 / math.sqrt(length))
    y = lax.all_to_all(y, "ctx", 0, 0, tiled=True)
    after = shifted(heads(y, qc, kc, vc, out_grad, skip), "ctx", -1)
    mixed_out, gq, gk, gv, rims, gf = spread(y, qc, kc, vc, out_grad, skip, taps_full)
    gq, gk, gv = tail(rims, after, taps_full, gq, gk, gv)
    return (mixed_out, gq, gk, gv, gf.T)


def solution(mesh):
    in_specs = (
        P("ctx", "tp"),
        P("ctx", "tp"),
        P("ctx", "tp"),
        P(None, None, "tp"),
        P("ctx", "tp"),
        P("tp"),
        P("ctx", "tp"),
    )
    out_specs = (P("ctx", "tp"),) * 5
    return jax.shard_map(body, mesh=mesh, in_specs=in_specs, out_specs=out_specs, check_vma=False)
```

time: 124 us -> 120 us (0.968)
  Pallas kernels: 26.7 us -> 24.5 us
  local copies, waits for them, and re-layouts: 2.78 us -> 0.69 us
  waiting for transfers between devices: 3.16 us -> 4.47 us
    ppermute x2, waiting for transfers between devices: 3.16 us -> 4.47 us  [shifted(): lax.ppermute(value, axis, [(source, source + steps) for source in range(i...]
    pallas_call x2 -> x3, Pallas kernels: 13.7 us -> 12.6 us  [the longest x1 5.93 us: spread(): pl.pallas_call(spread_kernel, grid=(width // cols,), in_specs=[resident]...]
where the time goes in v3:
time: 120 us; the launch traced here: 119 us
  blocking collectives  78.2 us (65%)
  Pallas kernels  24.5 us (20%)
  starting transfers between devices  10.9 us (9%)
  waiting for transfers between devices  4.47 us (4%)
    all_to_all x1, blocking collectives, body(): x = lax.all_to_all(x, 'ctx', 0, 0, tiled=True)  45.4 us
    all_to_all x1, blocking collectives, body(): y = lax.all_to_all(y, 'ctx', 0, 0, tiled=True)  32.8 us
    ppermute x2, starting transfers between devices, shifted(): lax.ppermute(value, axis, [(source, source + steps) for source in range(i...  10.9 us
    pallas_call x1, Pallas kernels, longconv(): pl.pallas_call(functools.partial(longconv_kernel, scale=scale), grid=(gro...  10 us
    pallas_call x1, Pallas kernels, spread(): pl.pallas_call(spread_kernel, grid=(width // cols,), in_specs=[resident]...  5.93 us
    pallas_call x1, Pallas kernels, featurize(): pl.pallas_call(featurize_kernel, grid=(width // cols,), in_specs=[tok, to...  5.9 us
    ppermute x2, waiting for transfers between devices, shifted(): lax.ppermute(value, axis, [(source, source + steps) for source in range(i...  4.47 us
  transfers between devices with their start and end apart: 2, of which 2 were waited for; matrix products, arithmetic and copies ran while one was open for 1% of the time, Pallas kernels for 5%

profile of v3, /device:TPU:38, one launch (start us, length us, event | category | flops | bytes accessed | tf_op | source)
XLA Modules:
  0.0 119.5 jit_solution(11757963576593006250)
XLA Ops:
  0.6 0.0 copy-start.2
  0.6 0.8 rims.1
  1.4 0.0 copy-start
  1.4 8.2 %collective-permute-start = (bf16[3,8,1024]{2,1,0:T(8,128)(2,1)S(1)}, bf16[3,8,1024]{2,1,0:T(8,128)(2,1)S(1)}, u32[]{:S(2)}, u32[]{:S(2)}) collective-permute-start(bf16[3,8,1024]{2,1,0:T(8,128)(2,1)S(1)} %rims.1), channel_id=1, source_target_pairs={{0,8},{8,16},{16,24},{24,32},{32,40},{40,48},{48,56},{56,64},{64,7... | collective-permute-start | bytes 147464 | tf_op jit(solution)/shard_map/ppermute | solution.py:30
  9.7 0.0 copy-done.2
  9.7 0.3 broadcast_in_dim.3
  10.0 0.4 reshape_reshape.3.taps_ref
  10.4 1.1 collective-permute-done.before_ref
  11.5 0.0 copy-done
  11.5 5.9 %featurize.1 = (bf16[32,72,256]{2,1,0:T(8,128)(2,1)}, f32[256,1024]{1,0:T(8,128)S(1)}, f32[256,1024]{1,0:T(8,128)S(1)}, f32[256,1024]{1,0:T(8,128)S(1)}) custom-call(bf16[256,1024]{1,0:T(8,128)(2,1)} %q_ref.3, bf16[256,1024]{1,0:T(8,128)(2,1)} %k_ref.3, bf16[256,1024]{1,0:T(8,128)(2,1)} %v_ref.3, bf16[256,1024]{1,0:T(8,128)(2,1)} %g_ref.5, ...), custom_call_target="tpu_custom_call" | custom-call | tf_op jit(solution)/shard_map/featurize/pallas_call | solution.py:125
  17.4 45.4 %all_to_all.10.x_ref = bf16[32,72,256]{2,1,0:T(8,128)(2,1)S(1)} all-to-all(bf16[32,72,256]{2,1,0:T(8,128)(2,1)} %get-tuple-element.18), channel_id=1, replica_groups=mesh['ctx'=32,'tp'=8] {'ctx'}, dimensions={0} | all-to-all | bytes 2359296 | tf_op jit(solution)/shard_map/all_to_all | solution.py:451
  62.8 10.0 %longconv.1 = bf16[32,72,256]{2,1,0:T(8,128)(2,1)} custom-call(bf16[32,72,256]{2,1,0:T(8,128)(2,1)S(1)} %all_to_all.10.x_ref), custom_call_target="tpu_custom_call" | custom-call | tf_op jit(solution)/shard_map/longconv/pallas_call | solution.py:272
  72.8 0.0 copy-start.1
  72.8 32.8 %all_to_all.11.y_ref = bf16[32,72,256]{2,1,0:T(8,128)(2,1)S(1)} all-to-all(bf16[32,72,256]{2,1,0:T(8,128)(2,1)} %longconv.1), channel_id=1, replica_groups=mesh['ctx'=32,'tp'=8] {'ctx'}, dimensions={0} | all-to-all | bytes 2359296 | tf_op jit(solution)/shard_map/all_to_all | solution.py:453
  105.7 0.0 copy-done.1
  105.7 1.0 heads.1
  106.7 2.7 %collective-permute-start.1 = (bf16[3,8,1024]{2,1,0:T(8,128)(2,1)S(1)}, bf16[3,8,1024]{2,1,0:T(8,128)(2,1)S(1)}, u32[]{:S(2)}, u32[]{:S(2)}) collective-permute-start(bf16[3,8,1024]{2,1,0:T(8,128)(2,1)S(1)} %heads.1), channel_id=1, source_target_pairs={{8,0},{16,8},{24,16},{32,24},{40,32},{48,40},{56,48},{64,56},{72,6... | collective-permute-start | bytes 147464 | tf_op jit(solution)/shard_map/ppermute | solution.py:30
  109.4 5.9 %spread.1 = (bf16[256,1024]{1,0:T(8,128)(2,1)}, bf16[256,1024]{1,0:T(8,128)(2,1)}, bf16[256,1024]{1,0:T(8,128)(2,1)}, bf16[256,1024]{1,0:T(8,128)(2,1)}, f32[3,1...) custom-call(bf16[32,72,256]{2,1,0:T(8,128)(2,1)S(1)} %all_to_all.11.y_ref, f32[256,1024]{1,0:T(8,128)S(1)} %get-tuple-element.19.qc_ref, ...), custom_call_target="tpu_custom_call" | custom-call | flops 12000000 | bytes 8000000 | tf_op jit(solution)/shard_map/spread/pallas_call | solution.py:386
  115.3 3.4 %collective-permute-done.1.after_ref = bf16[3,8,1024]{2,1,0:T(8,128)(2,1)S(1)} collective-permute-done((bf16[3,8,1024]{2,1,0:T(8,128)(2,1)S(1)}, bf16[3,8,1024]{2,1,0:T(8,128)(2,1)S(1)}, u32[]{:S(2)}, u32[]{:S(2)}) %collective-permute-start.1) | collective-permute-done | bytes 49184 | tf_op jit(solution)/shard_map/ppermute | solution.py:30
  118.7 0.8 tail.1
  (1 shorter events, 0.0 us)
Async XLA Ops:
  0.6 9.1 %copy-start.2 = (f32[3,7,64]{2,1,0:T(8,128)S(1)}, f32[3,7,64]{2,1,0:T(8,128)}, u32[]{:S(2)}) copy-start(f32[3,7,64]{2,1,0:T(8,128)} %param.10) | copy-start | bytes 16132
  1.4 10.1 %copy-start = (bf16[256,64]{0,1:T(8,128)(2,1)S(1)}, bf16[256,64]{0,1:T(8,128)(2,1)}, u32[]{:S(2)}) copy-start(bf16[256,64]{0,1:T(8,128)(2,1)} %param.11) | copy-start | bytes 98308
  1.4 10.1 %collective-permute-start = (bf16[3,8,1024]{2,1,0:T(8,128)(2,1)S(1)}, bf16[3,8,1024]{2,1,0:T(8,128)(2,1)S(1)}, u32[]{:S(2)}, u32[]{:S(2)}) collective-permute-start(bf16[3,8,1024]{2,1,0:T(8,128)(2,1)S(1)} %rims.1), channel_id=1, source_target_pairs={{0,8},{8,16},{16,24},{24,32},{32,40},{40,48},{48,56},{56,64},{64,7... | collective-permute-start | bytes 147464 | tf_op jit(solution)/shard_map/ppermute | solution.py:30
  72.8 32.8 %copy-start.1 = (f32[1024]{0:T(1024)S(1)}, f32[1024]{0:T(1024)}, u32[]{:S(2)}) copy-start(f32[1024]{0:T(1024)} %param.12) | copy-start | bytes 12292
  106.7 12.0 %collective-permute-start.1 = (bf16[3,8,1024]{2,1,0:T(8,128)(2,1)S(1)}, bf16[3,8,1024]{2,1,0:T(8,128)(2,1)S(1)}, u32[]{:S(2)}, u32[]{:S(2)}) collective-permute-start(bf16[3,8,1024]{2,1,0:T(8,128)(2,1)S(1)} %heads.1), channel_id=1, source_target_pairs={{8,0},{16,8},{24,16},{32,24},{40,32},{48,40},{56,48},{64,56},{72,6... | collective-permute-start | bytes 147464 | tf_op jit(solution)/shard_map/ppermute | solution.py:30

commit v4 on v3

--- a/solution.py
+++ b/solution.py
@@ -17,6 +17,7 @@
 COLS = 256
 CHUNK = 64
 SPARE = 8
+HALVES = 2
 LANES = 128
 VMEM_LIMIT = 30 * 1024 * 1024
 
@@ -101,14 +102,18 @@
             query_conv = conv(0)
             qc_ref[part, there] = query_conv
             mix[part, lanes] = (g_ref[part, lanes].astype(f32) * query_conv).astype(bf16)
-    x_ref[:, :half, :] = gated[...].T.reshape(owners, half, rows)
-    x_ref[:, half : 2 * half, :] = mix[...].T.reshape(owners, half, rows)
+    for which, signal in enumerate((gated, mix)):
+        for part in range(HALVES):
+            first = (HALVES * which + part) * half
+            piece = signal[LANES * part : LANES * (part + 1), :].T
+            x_ref[:, first : first + half, :] = piece.reshape(owners, half, LANES)
     lines = owners * owned_groups
     filt = f_ref[pl.ds(pl.multiple_of(pl.program_id(0) * lines, lines), lines), :].astype(f32)
-    blank = jnp.zeros((SPARE - owned_groups, rows), f32)
+    blank = jnp.zeros((SPARE - HALVES * owned_groups, LANES), f32)
     for owner in range(owners):
         mine = filt[owner * owned_groups : (owner + 1) * owned_groups]
-        x_ref[owner, 2 * half :, :] = jnp.concatenate([mine, blank], axis=0).astype(bf16)
+        pieces = [mine[:, LANES * part : LANES * (part + 1)] for part in range(HALVES)]
+        x_ref[owner, 2 * HALVES * half :, :] = jnp.concatenate([*pieces, blank], axis=0).astype(bf16)
 
 
 def in_hbm(*arrays):
@@ -118,7 +123,7 @@
 def featurize(query, key, value, grad, before, taps_full, filt, n_ctx):
     rows, width = query.shape
     owned = width // n_ctx
-    chunk = 2 * owned + SPARE
+    chunk = 2 * HALVES * owned + SPARE
     cols = COLS
     tok = pl.BlockSpec((rows, cols), lambda i: (0, i))
     resident = pl.BlockSpec(memory_space=pltpu.VMEM)
@@ -135,13 +140,13 @@
             resident,
         ],
         out_specs=[
-            pl.BlockSpec((cols // owned, chunk, rows), lambda i: (i, 0, 0)),
+            pl.BlockSpec((cols // owned, chunk, LANES), lambda i: (i, 0, 0)),
             resident,
             resident,
             resident,
         ],
         out_shape=[
-            pltpu.HBM((n_ctx, chunk, rows), bf16),
+            pltpu.HBM((n_ctx, chunk, LANES), bf16),
             jax.ShapeDtypeStruct((rows, width), f32),
             jax.ShapeDtypeStruct((rows, width), f32),
             jax.ShapeDtypeStruct((rows, width), f32),
@@ -175,8 +180,9 @@
 
 def longconv_kernel(x_ref, y_hbm, fpad, toe, gpad, zpad, acc, corr, fgrad, y_ref, sems, *, scale):
     g = pl.program_id(0)
-    blocks, chunk, size = x_ref.shape
-    half = (chunk - SPARE) // 2
+    blocks, chunk, _ = x_ref.shape
+    size = HALVES * LANES
+    half = (chunk - SPARE) // (2 * HALVES)
     length = blocks * size
     rows = blocks * GROUP
     group = GROUP
@@ -188,16 +194,35 @@
     def _():
         fpad[:, : 2 * LANES] = jnp.zeros((SPARE, 2 * LANES), f32)
         for j in range(blocks):
-            lo = 2 * LANES + size * j
-            fpad[:, lo : lo + size] = x_ref[j, 2 * half :, :].astype(f32)
+            spare = x_ref[j, 2 * HALVES * half :, :].astype(f32)
+            for part in range(HALVES):
+                lo = 2 * LANES + size * j + LANES * part
+                fpad[:groups, lo : lo + LANES] = spare[groups * part : groups * (part + 1)]
         fgrad[...] = jnp.zeros_like(fgrad)
 
     build_toeplitz(fpad, g, length, toe)
     gpad[:top, :] = jnp.zeros((top, size), bf16)
-    lines = pl.ds(pl.multiple_of(g * group, group), group)
-    back_lines = pl.ds(pl.multiple_of(half + g * group, group), group)
-    gpad[top:, :] = x_ref[:, lines, :].reshape(rows, size)
-    zpad[:rows, :] = x_ref[:, back_lines, :].reshape(rows, size)
+
+    def lines(which, part):
+        return pl.ds(pl.multiple_of((HALVES * which + part) * half + g * group, group), group)
+
+    def put(which):
+        for part in range(HALVES):
+            piece = (acc[:, LANES * part : LANES * (part + 1)] * scale).astype(bf16)
+            place = lines(which, part)
+            y_ref[:, place, :] = piece.reshape(blocks, group, LANES)
+            copy(g, which, part).start()
+
+    def copy(i, which, part):
+        place = pl.ds(pl.multiple_of((HALVES * which + part) * half + i * group, group), group)
+        return pltpu.make_async_copy(
+            y_ref.at[:, place, :], y_hbm.at[:, place, :], sems.at[i, HALVES * which + part]
+        )
+
+    for part in range(HALVES):
+        lanes = slice(LANES * part, LANES * (part + 1))
+        gpad[top:, lanes] = x_ref[:, lines(0, part), :].reshape(rows, LANES)
+        zpad[:rows, lanes] = x_ref[:, lines(1, part), :].reshape(rows, LANES)
     zpad[rows:, :] = jnp.zeros((zpad.shape[0] - rows, size), bf16)
 
     u_t = gpad[top:, :].astype(f32).T.astype(bf16)
@@ -233,9 +258,7 @@
         right = jnp.concatenate([toeplitz_rows(batch * kb + i, size) for i in range(batch)], axis=0)
         part = jnp.dot(left[: rows - first], right, preferred_element_type=f32)
         acc[first:, :] = part if kb == 0 else acc[first:, :] + part
-    y_ref[:, lines, :] = (acc[...] * scale).astype(bf16).reshape(blocks, group, size)
-    conv_out = pltpu.make_async_copy(y_ref.at[:, lines, :], y_hbm.at[:, lines, :], sems.at[g, 0])
-    conv_out.start()
+    put(0)
 
     for kb in range(blocks // batch):
         first = top * kb
@@ -246,29 +269,33 @@
         )
         part = lax.dot_general(left, right, (((1,), (1,)), ((), ())), preferred_element_type=f32)
         acc[:count, :] = part if kb == 0 else acc[:count, :] + part
-    y_ref[:, back_lines, :] = (acc[...] * scale).astype(bf16).reshape(blocks, group, size)
-    back_out = pltpu.make_async_copy(y_ref.at[:, back_lines, :], y_hbm.at[:, back_lines, :], sems.at[g, 1])
-    back_out.start()
+    put(1)
 
     @pl.when(g == groups - 1)
     def _():
+        blank = jnp.zeros((SPARE - HALVES * groups, LANES), f32)
         for j in range(blocks):
-            y_ref[j, 2 * half :, :] = fgrad[:, size * j : size * (j + 1)].astype(bf16)
-        spare = pl.ds(2 * half, SPARE)
-        spare_out = pltpu.make_async_copy(y_ref.at[:, spare, :], y_hbm.at[:, spare, :], sems.at[0, 2])
+            starts = [size * j + LANES * part for part in range(HALVES)]
+            pieces = [fgrad[:groups, lo : lo + LANES] for lo in starts]
+            y_ref[j, 2 * HALVES * half :, :] = jnp.concatenate([*pieces, blank], axis=0).astype(bf16)
+        spare = pl.ds(2 * HALVES * half, SPARE)
+        spare_out = pltpu.make_async_copy(
+            y_ref.at[:, spare, :], y_hbm.at[:, spare, :], sems.at[0, 2 * HALVES]
+        )
         spare_out.start()
         for i in range(groups):
-            for k, first in enumerate((0, half)):
-                part = pl.ds(first + i * group, group)
-                pltpu.make_async_copy(y_ref.at[:, part, :], y_hbm.at[:, part, :], sems.at[i, k]).wait()
+            for which in range(2):
+                for part in range(HALVES):
+                    copy(i, which, part).wait()
         spare_out.wait()
 
 
 def longconv(x, scale):
-    blocks, chunk, size = x.shape
+    blocks, chunk, _ = x.shape
+    size = HALVES * LANES
     length = blocks * size
     rows = blocks * GROUP
-    groups = (chunk - SPARE) // 2 // GROUP
+    groups = (chunk - SPARE) // (2 * HALVES) // GROUP
     return pl.pallas_call(
         functools.partial(longconv_kernel, scale=scale),
         grid=(groups,),
@@ -284,16 +311,16 @@
             pltpu.VMEM((size, length + 2 * LANES), f32),
             pltpu.VMEM((SPARE, length), f32),
             pltpu.VMEM(x.shape, bf16),
-            pltpu.SemaphoreType.DMA((groups, 3)),
+            pltpu.SemaphoreType.DMA((groups, 2 * HALVES + 1)),
         ],
         compiler_params=pltpu.CompilerParams(vmem_limit_bytes=VMEM_LIMIT),
         name="longconv",
     )(x)
 
 
-def tokens(y_ref, lo, count, lanes):
+def tokens(y_ref, block, count):
     owners = y_ref.shape[0]
-    return y_ref[:, lo : lo + count, :lanes].reshape(owners * count, lanes).T
+    return y_ref[:, block * count : (block + 1) * count, :].reshape(owners * count, LANES).T
 
 
 def grads(conv, back, qc, kc, vc, grad, skip):
@@ -305,9 +332,9 @@
 
 
 def heads_kernel(y_ref, qc_ref, kc_ref, vc_ref, g_ref, skip_ref, out_ref):
-    half = (y_ref.shape[1] - SPARE) // 2
-    conv = tokens(y_ref, 0, half, LANES).astype(f32)[:HALO]
-    back = tokens(y_ref, half, half, LANES).astype(f32)[:HALO]
+    half = (y_ref.shape[1] - SPARE) // (2 * HALVES)
+    conv = tokens(y_ref, 0, half).astype(f32)[:HALO]
+    back = tokens(y_ref, HALVES, half).astype(f32)[:HALO]
     grad = g_ref[...].astype(f32)[:HALO]
     _, gq, gk, gv = grads(conv, back, qc_ref[...], kc_ref[...], vc_ref[...], grad, skip_ref[...])
     out_ref[0] = gq.astype(bf16)
@@ -316,7 +343,7 @@
 
 
 def heads(y, qc, kc, vc, grad, skip):
-    n_ctx, chunk, rows = y.shape
+    n_ctx, chunk, _ = y.shape
     width = qc.shape[1]
     cols = 512
     top = pl.BlockSpec((HALO, cols), lambda i: (0, i))
@@ -342,15 +369,20 @@
     y_ref, qc_ref, kc_ref, vc_ref, g_ref, skip_ref, taps_ref, out_ref, gq_ref, gk_ref, gv_ref, tail_ref, gf_ref, conv, back, ext
 ):
     rows, cols = g_ref.shape
-    half = (y_ref.shape[1] - SPARE) // 2
+    half = (y_ref.shape[1] - SPARE) // (2 * HALVES)
     owners = cols // half
     owned_groups = gf_ref.shape[0] // owners
     step = pl.program_id(0)
     y_ref = y_ref.at[pl.ds(step * owners, owners)]
-    lines = [y_ref[o, 2 * half :, :].astype(f32)[:owned_groups] for o in range(owners)]
+    lines = []
+    for owner in range(owners):
+        spare = y_ref[owner, 2 * HALVES * half :, :].astype(f32)
+        pieces = [spare[owned_groups * part : owned_groups * (part + 1)] for part in range(HALVES)]
+        lines.append(jnp.concatenate(pieces, axis=1))
     gf_ref[...] = jnp.concatenate(lines, axis=0).astype(bf16)
-    conv[...] = tokens(y_ref, 0, half, rows)
-    back[...] = tokens(y_ref, half, half, rows)
+    for part in range(HALVES):
+        conv[LANES * part : LANES * (part + 1), :] = tokens(y_ref, part, half)
+        back[LANES * part : LANES * (part + 1), :] = tokens(y_ref, HALVES + part, half)
     for which in range(3):
         ext[which, rows:, :] = jnp.zeros((HALO, cols), f32)
     for left in range(0, cols, LANES):
@@ -378,8 +410,7 @@
 
 
 def spread(y, qc, kc, vc, grad, skip, taps_full):
-    n_ctx, chunk, rows = y.shape
-    width = qc.shape[1]
+    rows, width = qc.shape
     cols = COLS
     tok = pl.BlockSpec((rows, cols), lambda i: (0, i))
     resident = pl.BlockSpec(memory_space=pltpu.VMEM)

time: 120 us -> 117 us (0.975)
  blocking collectives: 78.2 us -> 75.1 us
    all_to_all x1, blocking collectives: 32.8 us -> 30.8 us  [body(): y = lax.all_to_all(y, 'ctx', 0, 0, tiled=True)]
where the time goes in v4:
time: 117 us; the launch traced here: 116 us
  blocking collectives  75.1 us (64%)
  Pallas kernels  24.4 us (21%)
  starting transfers between devices  10.7 us (9%)
  waiting for transfers between devices  4.75 us (4%)
    all_to_all x1, blocking collectives, body(): x = lax.all_to_all(x, 'ctx', 0, 0, tiled=True)  44.3 us
    all_to_all x1, blocking collectives, body(): y = lax.all_to_all(y, 'ctx', 0, 0, tiled=True)  30.8 us
    ppermute x2, starting transfers between devices, shifted(): lax.ppermute(value, axis, [(source, source + steps) for source in range(i...  10.7 us
    pallas_call x1, Pallas kernels, longconv(): pl.pallas_call(functools.partial(longconv_kernel, scale=scale), grid=(gro...  10 us
    pallas_call x1, Pallas kernels, featurize(): pl.pallas_call(featurize_kernel, grid=(width // cols,), in_specs=[tok, to...  5.88 us
    pallas_call x1, Pallas kernels, spread(): pl.pallas_call(spread_kernel, grid=(width // cols,), in_specs=[resident]...  5.86 us
    ppermute x2, waiting for transfers between devices, shifted(): lax.ppermute(value, axis, [(source, source + steps) for source in range(i...  4.75 us
  transfers between devices with their start and end apart: 2, of which 2 were waited for; matrix products, arithmetic and copies ran while one was open for 1% of the time, Pallas kernels for 5%

profile of v4, /device:TPU:38, one launch (start us, length us, event | category | flops | bytes accessed | tf_op | source)
XLA Modules:
  0.0 116.3 jit_solution(16917575223587179278)
XLA Ops:
  0.6 0.0 copy-start.2
  0.6 0.8 rims.1
  1.4 0.0 copy-start
  1.4 8.2 %collective-permute-start = (bf16[3,8,1024]{2,1,0:T(8,128)(2,1)S(1)}, bf16[3,8,1024]{2,1,0:T(8,128)(2,1)S(1)}, u32[]{:S(2)}, u32[]{:S(2)}) collective-permute-start(bf16[3,8,1024]{2,1,0:T(8,128)(2,1)S(1)} %rims.1), channel_id=1, source_target_pairs={{0,8},{8,16},{16,24},{24,32},{32,40},{40,48},{48,56},{56,64},{64,7... | collective-permute-start | bytes 147464 | tf_op jit(solution)/shard_map/ppermute | solution.py:31
  9.7 0.0 copy-done.2
  9.7 0.3 broadcast_in_dim.3
  10.0 0.4 reshape_reshape.3.taps_ref
  10.4 1.1 collective-permute-done.before_ref
  11.5 0.0 copy-done
  11.5 5.9 %featurize.1 = (bf16[32,136,128]{2,1,0:T(8,128)(2,1)}, f32[256,1024]{1,0:T(8,128)S(1)}, f32[256,1024]{1,0:T(8,128)S(1)}, f32[256,1024]{1,0:T(8,128)S(1)}) custom-call(bf16[256,1024]{1,0:T(8,128)(2,1)} %q_ref.3, bf16[256,1024]{1,0:T(8,128)(2,1)} %k_ref.3, bf16[256,1024]{1,0:T(8,128)(2,1)} %v_ref.3, bf16[256,1024]{1,0:T(8,128)(2,1)} %g_ref.5, ...), custom_call_target="tpu_custom_call" | custom-call | tf_op jit(solution)/shard_map/featurize/pallas_call | solution.py:130
  17.4 44.3 %all_to_all.10.x_ref = bf16[32,136,128]{2,1,0:T(8,128)(2,1)S(1)} all-to-all(bf16[32,136,128]{2,1,0:T(8,128)(2,1)} %get-tuple-element.18), channel_id=1, replica_groups=mesh['ctx'=32,'tp'=8] {'ctx'}, dimensions={0} | all-to-all | bytes 2228224 | tf_op jit(solution)/shard_map/all_to_all | solution.py:482
  61.7 10.0 %longconv.1 = bf16[32,136,128]{2,1,0:T(8,128)(2,1)} custom-call(bf16[32,136,128]{2,1,0:T(8,128)(2,1)S(1)} %all_to_all.10.x_ref), custom_call_target="tpu_custom_call" | custom-call | tf_op jit(solution)/shard_map/longconv/pallas_call | solution.py:299
  71.7 0.0 copy-start.1
  71.7 30.8 %all_to_all.11.y_ref = bf16[32,136,128]{2,1,0:T(8,128)(2,1)S(1)} all-to-all(bf16[32,136,128]{2,1,0:T(8,128)(2,1)} %longconv.1), channel_id=1, replica_groups=mesh['ctx'=32,'tp'=8] {'ctx'}, dimensions={0} | all-to-all | bytes 2228224 | tf_op jit(solution)/shard_map/all_to_all | solution.py:484
  102.5 0.0 copy-done.1
  102.5 0.9 heads.1
  103.5 2.5 %collective-permute-start.1 = (bf16[3,8,1024]{2,1,0:T(8,128)(2,1)S(1)}, bf16[3,8,1024]{2,1,0:T(8,128)(2,1)S(1)}, u32[]{:S(2)}, u32[]{:S(2)}) collective-permute-start(bf16[3,8,1024]{2,1,0:T(8,128)(2,1)S(1)} %heads.1), channel_id=1, source_target_pairs={{8,0},{16,8},{24,16},{32,24},{40,32},{48,40},{56,48},{64,56},{72,6... | collective-permute-start | bytes 147464 | tf_op jit(solution)/shard_map/ppermute | solution.py:31
  106.0 5.9 %spread.1 = (bf16[256,1024]{1,0:T(8,128)(2,1)}, bf16[256,1024]{1,0:T(8,128)(2,1)}, bf16[256,1024]{1,0:T(8,128)(2,1)}, bf16[256,1024]{1,0:T(8,128)(2,1)}, f32[3,1...) custom-call(bf16[32,136,128]{2,1,0:T(8,128)(2,1)S(1)} %all_to_all.11.y_ref, f32[256,1024]{1,0:T(8,128)S(1)} %get-tuple-element.19.qc_ref, ...), custom_call_target="tpu_custom_call" | custom-call | flops 12000000 | bytes 8000000 | tf_op jit(solution)/shard_map/spread/pallas_call | solution.py:417
  111.9 3.6 %collective-permute-done.1.after_ref = bf16[3,8,1024]{2,1,0:T(8,128)(2,1)S(1)} collective-permute-done((bf16[3,8,1024]{2,1,0:T(8,128)(2,1)S(1)}, bf16[3,8,1024]{2,1,0:T(8,128)(2,1)S(1)}, u32[]{:S(2)}, u32[]{:S(2)}) %collective-permute-start.1) | collective-permute-done | bytes 49184 | tf_op jit(solution)/shard_map/ppermute | solution.py:31
  115.5 0.8 tail.1
  (1 shorter events, 0.0 us)
Async XLA Ops:
  0.6 9.1 %copy-start.2 = (f32[3,7,64]{2,1,0:T(8,128)S(1)}, f32[3,7,64]{2,1,0:T(8,128)}, u32[]{:S(2)}) copy-start(f32[3,7,64]{2,1,0:T(8,128)} %param.10) | copy-start | bytes 16132
  1.4 10.1 %copy-start = (bf16[256,64]{0,1:T(8,128)(2,1)S(1)}, bf16[256,64]{0,1:T(8,128)(2,1)}, u32[]{:S(2)}) copy-start(bf16[256,64]{0,1:T(8,128)(2,1)} %param.11) | copy-start | bytes 98308
  1.4 10.1 %collective-permute-start = (bf16[3,8,1024]{2,1,0:T(8,128)(2,1)S(1)}, bf16[3,8,1024]{2,1,0:T(8,128)(2,1)S(1)}, u32[]{:S(2)}, u32[]{:S(2)}) collective-permute-start(bf16[3,8,1024]{2,1,0:T(8,128)(2,1)S(1)} %rims.1), channel_id=1, source_target_pairs={{0,8},{8,16},{16,24},{24,32},{32,40},{40,48},{48,56},{56,64},{64,7... | collective-permute-start | bytes 147464 | tf_op jit(solution)/shard_map/ppermute | solution.py:31
  71.7 30.8 %copy-start.1 = (f32[1024]{0:T(1024)S(1)}, f32[1024]{0:T(1024)}, u32[]{:S(2)}) copy-start(f32[1024]{0:T(1024)} %param.12) | copy-start | bytes 12292
  103.5 12.0 %collective-permute-start.1 = (bf16[3,8,1024]{2,1,0:T(8,128)(2,1)S(1)}, bf16[3,8,1024]{2,1,0:T(8,128)(2,1)S(1)}, u32[]{:S(2)}, u32[]{:S(2)}) collective-permute-start(bf16[3,8,1024]{2,1,0:T(8,128)(2,1)S(1)} %heads.1), channel_id=1, source_target_pairs={{8,0},{16,8},{24,16},{32,24},{40,32},{48,40},{56,48},{64,56},{72,6... | collective-permute-start | bytes 147464 | tf_op jit(solution)/shard_map/ppermute | solution.py:31

commit v5 on v4

--- a/solution.py
+++ b/solution.py
@@ -13,13 +13,13 @@
 GROUP = D // SHORT_GROUPS
 TAPS = 7
 HALO = 8
-TAIL = 16
+STRIP = 16
 COLS = 256
 CHUNK = 64
 SPARE = 8
 HALVES = 2
 LANES = 128
-VMEM_LIMIT = 30 * 1024 * 1024
+VMEM_LIMIT = 24 * 1024 * 1024
 
 f32 = jnp.float32
 bf16 = jnp.bfloat16
@@ -31,24 +31,34 @@
     return lax.ppermute(value, axis, [(source, source + steps) for source in range(initial, last)])
 
 
-def rims_kernel(q_ref, k_ref, v_ref, out_ref):
-    for which, ref in enumerate((q_ref, k_ref, v_ref)):
-        out_ref[which] = ref[...].astype(f32)[HALO:].astype(bf16)
-
-
-def last_rows(query, key, value):
+def rims_kernel(*refs):
+    *ends, last_ref, first_ref = refs
+    for which, ref in enumerate(ends[:3]):
+        last_ref[which] = ref[...].astype(f32)[HALO:].astype(bf16)
+    for which, ref in enumerate(ends[3:]):
+        first_ref[which] = ref[...].astype(f32)[:HALO].astype(bf16)
+
+
+def rims(query, key, value, grad):
     rows, width = query.shape
-    last = rows // TAIL - 1
-    strip = pl.BlockSpec((TAIL, width), lambda i: (last, 0))
+    end = rows // STRIP - 1
+    last = pl.BlockSpec((STRIP, width), lambda i: (end, 0))
+    first = pl.BlockSpec((STRIP, width), lambda i: (0, 0))
     return pl.pallas_call(
         rims_kernel,
         grid=(1,),
-        in_specs=[strip] * 3,
-        out_specs=pl.BlockSpec((3, HALO, width), lambda i: (0, 0, 0)),
-        out_shape=jax.ShapeDtypeStruct((3, HALO, width), bf16),
+        in_specs=[last] * 3 + [first] * 4,
+        out_specs=[
+            pl.BlockSpec((3, HALO, width), lambda i: (0, 0, 0)),
+            pl.BlockSpec((4, HALO, width), lambda i: (0, 0, 0)),
+        ],
+        out_shape=[
+            jax.ShapeDtypeStruct((3, HALO, width), bf16),
+            jax.ShapeDtypeStruct((4, HALO, width), bf16),
+        ],
         compiler_params=pltpu.CompilerParams(vmem_limit_bytes=VMEM_LIMIT),
         name="rims",
-    )(*in_hbm(query, key, value))
+    )(*in_hbm(query, key, value, query, key, value, grad))
 
 
 def widen(short_taps):
@@ -97,7 +107,7 @@
             key_conv = conv(1)
             kc_ref[part, there] = key_conv
             value_conv = conv(2)
-            vc_ref[part, there] = value_conv
+            vc_ref[part, lanes] = value_conv
             gated[part, lanes] = (key_conv * value_conv).astype(bf16)
             query_conv = conv(0)
             qc_ref[part, there] = query_conv
@@ -143,13 +153,13 @@
             pl.BlockSpec((cols // owned, chunk, LANES), lambda i: (i, 0, 0)),
             resident,
             resident,
-            resident,
+            tok,
         ],
         out_shape=[
             pltpu.HBM((n_ctx, chunk, LANES), bf16),
             jax.ShapeDtypeStruct((rows, width), f32),
             jax.ShapeDtypeStruct((rows, width), f32),
-            jax.ShapeDtypeStruct((rows, width), f32),
+            pltpu.HBM((rows, width), f32),
         ],
         scratch_shapes=[
             pltpu.VMEM((3, rows + HALO, cols), f32),
@@ -178,7 +188,7 @@
             toe[p : p + 16, lo + LANES : lo + LANES + WIDE // 2] = wide[:, LANES:].astype(bf16)
 
 
-def longconv_kernel(x_ref, y_hbm, fpad, toe, gpad, zpad, acc, corr, fgrad, y_ref, sems, *, scale):
+def longconv_kernel(x_ref, y_hbm, fpad, toe, gpad, zpad, acc, corr, fgrad, ahead, y_ref, sems, *, scale):
     g = pl.program_id(0)
     blocks, chunk, _ = x_ref.shape
     size = HALVES * LANES
@@ -273,11 +283,27 @@
 
     @pl.when(g == groups - 1)
     def _():
-        blank = jnp.zeros((SPARE - HALVES * groups, LANES), f32)
+        bits = group.bit_length() - 1
+        token = lax.broadcasted_iota(jnp.int32, (LANES, LANES), 0)
+        lane = lax.broadcasted_iota(jnp.int32, (LANES, LANES), 1)
+        spot = ((lane >> bits) == HALO - 1 - token).astype(f32).astype(bf16)
+        channel = lax.broadcasted_iota(jnp.int32, (group, LANES), 0)
+        own = (lax.broadcasted_iota(jnp.int32, (group, LANES), 1) & (group - 1)) == channel
+        block = lax.broadcasted_iota(jnp.int32, (blocks, rows), 1) >> bits
+        after = (block == lax.broadcasted_iota(jnp.int32, (blocks, rows), 0) + 1).astype(f32).astype(bf16)
+        for which in range(2):
+            for i in range(groups):
+                first = HALVES * which * half + i * group
+                piece = y_ref[:, first : first + group, :].reshape(rows, LANES)
+                tall = jnp.dot(piece, spot, preferred_element_type=f32).reshape(blocks, group, LANES)
+                tall = jnp.where(own[None], tall, 0.0).reshape(rows, LANES).astype(bf16)
+                place = (which * groups + i) * blocks
+                ahead[place : place + blocks, :] = jnp.dot(after, tall, preferred_element_type=f32)
         for j in range(blocks):
             starts = [size * j + LANES * part for part in range(HALVES)]
             pieces = [fgrad[:groups, lo : lo + LANES] for lo in starts]
-            y_ref[j, 2 * HALVES * half :, :] = jnp.concatenate([*pieces, blank], axis=0).astype(bf16)
+            pieces += [ahead[blocks * i + j : blocks * i + j + 1, :] for i in range(2 * groups)]
+            y_ref[j, 2 * HALVES * half :, :] = jnp.concatenate(pieces, axis=0).astype(bf16)
         spare = pl.ds(2 * HALVES * half, SPARE)
         spare_out = pltpu.make_async_copy(
             y_ref.at[:, spare, :], y_hbm.at[:, spare, :], sems.at[0, 2 * HALVES]
@@ -310,6 +336,7 @@
             pltpu.VMEM((rows, size), f32),
             pltpu.VMEM((size, length + 2 * LANES), f32),
             pltpu.VMEM((SPARE, length), f32),
+            pltpu.VMEM((2 * groups * blocks, LANES), f32),
             pltpu.VMEM(x.shape, bf16),
             pltpu.SemaphoreType.DMA((groups, 2 * HALVES + 1)),
         ],
@@ -331,42 +358,24 @@
     return mixed, grad * mixed, grad_gate * vc, grad_gate * kc
 
 
-def heads_kernel(y_ref, qc_ref, kc_ref, vc_ref, g_ref, skip_ref, out_ref):
-    half = (y_ref.shape[1] - SPARE) // (2 * HALVES)
-    conv = tokens(y_ref, 0, half).astype(f32)[:HALO]
-    back = tokens(y_ref, HALVES, half).astype(f32)[:HALO]
-    grad = g_ref[...].astype(f32)[:HALO]
-    _, gq, gk, gv = grads(conv, back, qc_ref[...], kc_ref[...], vc_ref[...], grad, skip_ref[...])
-    out_ref[0] = gq.astype(bf16)
-    out_ref[1] = gk.astype(bf16)
-    out_ref[2] = gv.astype(bf16)
-
-
-def heads(y, qc, kc, vc, grad, skip):
-    n_ctx, chunk, _ = y.shape
-    width = qc.shape[1]
-    cols = 512
-    top = pl.BlockSpec((HALO, cols), lambda i: (0, i))
-    return pl.pallas_call(
-        heads_kernel,
-        grid=(width // cols,),
-        in_specs=[
-            pl.BlockSpec((cols * n_ctx // width, chunk, LANES), lambda i: (i, 0, 0)),
-            top,
-            top,
-            top,
-            pl.BlockSpec((2 * HALO, cols), lambda i: (0, i)),
-            pl.BlockSpec((1, cols), lambda i: (0, i)),
-        ],
-        out_specs=pl.BlockSpec((3, HALO, cols), lambda i: (0, 0, i)),
-        out_shape=jax.ShapeDtypeStruct((3, HALO, width), bf16),
-        compiler_params=pltpu.CompilerParams(vmem_limit_bytes=VMEM_LIMIT),
-        name="heads",
-    )(y, qc, kc, vc, *in_hbm(grad), skip)
+def unpacked(lines):
+    shape = (HALO, LANES)
+    lane = lax.broadcasted_iota(jnp.int32, shape, 1)
+    token = lax.broadcasted_iota(jnp.int32, shape, 0)
+    total = jnp.zeros(shape, f32)
+    for r, line in enumerate(lines):
+        base = GROUP * ((r + 1) % HALO)
+        moved = jnp.broadcast_to(line, shape)
+        moved = pltpu.roll(moved, base, axis=1) if base else moved
+        for bit in (1, 2, 4):
+            moved = jnp.where((token & bit) != 0, pltpu.roll(moved, GROUP * bit, axis=1), moved)
+        total = jnp.where(lane // GROUP == r, moved, total)
+    return total
 
 
 def spread_kernel(
-    y_ref, qc_ref, kc_ref, vc_ref, g_ref, skip_ref, taps_ref, out_ref, gq_ref, gk_ref, gv_ref, tail_ref, gf_ref, conv, back, ext
+    y_ref, qc_ref, kc_ref, vc_ref, g_ref, skip_ref, taps_ref, last_ref, next_ref,
+    out_ref, gq_ref, gk_ref, gv_ref, gf_ref, conv, back, ext, edge,
 ):
     rows, cols = g_ref.shape
     half = (y_ref.shape[1] - SPARE) // (2 * HALVES)
@@ -374,21 +383,34 @@
     owned_groups = gf_ref.shape[0] // owners
     step = pl.program_id(0)
     y_ref = y_ref.at[pl.ds(step * owners, owners)]
-    lines = []
+    lines, ends = [], []
     for owner in range(owners):
         spare = y_ref[owner, 2 * HALVES * half :, :].astype(f32)
         pieces = [spare[owned_groups * part : owned_groups * (part + 1)] for part in range(HALVES)]
         lines.append(jnp.concatenate(pieces, axis=1))
+        ends.append(spare[HALVES * owned_groups :])
     gf_ref[...] = jnp.concatenate(lines, axis=0).astype(bf16)
     for part in range(HALVES):
         conv[LANES * part : LANES * (part + 1), :] = tokens(y_ref, part, half)
         back[LANES * part : LANES * (part + 1), :] = tokens(y_ref, HALVES + part, half)
-    for which in range(3):
-        ext[which, rows:, :] = jnp.zeros((HALO, cols), f32)
     for left in range(0, cols, LANES):
         lanes = slice(left, left + LANES)
         there = pl.ds(pl.multiple_of(step * cols + left, LANES), LANES)
         taps = [tap_rows(taps_ref, which, there) for which in range(3)]
+        after = []
+        for which in range(3):
+            edge[which, :HALO, :] = last_ref[which, :, there].astype(f32)
+            edge[which, HALO:, :] = next_ref[which, :, there].astype(f32)
+            after.append(weighted(taps[which], [edge[which, HALO - j : 2 * HALO - j, :] for j in range(TAPS)]))
+        first = left // GROUP
+        tile = [divmod(first + r, owned_groups) for r in range(LANES // GROUP)]
+        conv_next, back_next = [
+            unpacked([ends[o][owned_groups * kind + i : owned_groups * kind + i + 1] for o, i in tile])
+            for kind in range(2)
+        ]
+        _, *signals = grads(conv_next, back_next, *after, next_ref[3, :, there].astype(f32), skip_ref[:, there])
+        for which in range(3):
+            ext[which, rows:, lanes] = signals[which]
         for lo in reversed(range(0, rows, CHUNK)):
             part = slice(lo, lo + CHUNK)
             qc = qc_ref[part, there]
@@ -397,7 +419,7 @@
                 back[part, lanes].astype(f32),
                 qc,
                 kc_ref[part, there],
-                vc_ref[part, there],
+                vc_ref[part, lanes],
                 g_ref[part, lanes].astype(f32),
                 skip_ref[:, there],
             )
@@ -406,10 +428,9 @@
                 ext[which, part, lanes] = signals[which]
                 pieces = [ext[which, lo + j : lo + j + CHUNK, lanes] for j in range(TAPS)]
                 target[part, lanes] = weighted(taps[which], pieces).astype(bf16)
-    tail_ref[...] = ext[:, rows - TAIL : rows, :]
-
-
-def spread(y, qc, kc, vc, grad, skip, taps_full):
+
+
+def spread(y, qc, kc, vc, grad, skip, taps_full, last, following):
     rows, width = qc.shape
     cols = COLS
     tok = pl.BlockSpec((rows, cols), lambda i: (0, i))
@@ -417,58 +438,23 @@
     return pl.pallas_call(
         spread_kernel,
         grid=(width // cols,),
-        in_specs=[resident] * 4 + [tok] + [resident] * 2,
+        in_specs=[resident] * 3 + [tok] * 2 + [resident] * 4,
         out_specs=[tok] * 4
         + [
-            pl.BlockSpec((3, TAIL, cols), lambda i: (0, 0, i)),
             pl.BlockSpec((cols // GROUP, rows), lambda i: (i, 0)),
         ],
         out_shape=[jax.ShapeDtypeStruct((rows, width), bf16)] * 4
-        + [jax.ShapeDtypeStruct((3, TAIL, width), f32), jax.ShapeDtypeStruct((width // GROUP, rows), bf16)],
+        + [jax.ShapeDtypeStruct((width // GROUP, rows), bf16)],
         scratch_shapes=[
             pltpu.VMEM((rows, cols), bf16),
             pltpu.VMEM((rows, cols), bf16),
             pltpu.VMEM((3, rows + HALO, cols), f32),
+            pltpu.VMEM((3, 2 * HALO, LANES), f32),
         ],
         compiler_params=pltpu.CompilerParams(vmem_limit_bytes=VMEM_LIMIT),
         cost_estimate=pl.CostEstimate(flops=12_000_000, bytes_accessed=8_000_000, transcendentals=0),
         name="spread",
-    )(y, qc, kc, vc, *in_hbm(grad), skip, taps_full)
-
-
-def tail_kernel(tail_ref, after_ref, taps_ref, gq_in, gk_in, gv_in, gq_ref, gk_ref, gv_ref, ext):
-    ext[:, :TAIL, :] = tail_ref[...]
-    ext[:, TAIL:, :] = after_ref[...].astype(f32)
-    for which, target in enumerate((gq_ref, gk_ref, gv_ref)):
-        for left in range(0, ext.shape[2], LANES):
-            lanes = slice(left, left + LANES)
-            pieces = [ext[which, j : j + TAIL, lanes] for j in range(TAPS)]
-            target[:, lanes] = weighted(tap_rows(taps_ref, which, lanes), pieces).astype(bf16)
-
-
-def tail(rims, after, taps_full, gq, gk, gv):
-    rows, width = gq.shape
-    last = rows // TAIL - 1
-    strip = pl.BlockSpec((TAIL, width), lambda i: (last, 0))
-    anywhere = pl.BlockSpec(memory_space=pl.ANY)
-    return pl.pallas_call(
-        tail_kernel,
-        grid=(1,),
-        in_specs=[
-            pl.BlockSpec(rims.shape, lambda i: (0, 0, 0)),
-            pl.BlockSpec(after.shape, lambda i: (0, 0, 0)),
-            pl.BlockSpec(taps_full.shape, lambda i: (0, 0)),
-            anywhere,
-            anywhere,
-            anywhere,
-        ],
-        out_specs=[strip] * 3,
-        out_shape=[jax.ShapeDtypeStruct(gq.shape, bf16)] * 3,
-        scratch_shapes=[pltpu.VMEM((3, TAIL + HALO, width), f32)],
-        input_output_aliases={3: 0, 4: 1, 5: 2},
-        compiler_params=pltpu.CompilerParams(vmem_limit_bytes=VMEM_LIMIT),
-        name="tail",
-    )(rims, after, taps_full, gq, gk, gv)
+    )(y, qc, kc, vc, *in_hbm(grad), skip, taps_full, last, following)
 
 
 def body(query_feats, key_feats, value_feats, short_taps, long_filter, skip_gain, out_grad):
@@ -477,14 +463,14 @@
     length = tok_rows * n_ctx
     taps_full = widen(short_taps)
     skip = skip_gain.reshape(1, width)
-    before = shifted(last_rows(query_feats, key_feats, value_feats), "ctx", 1)
+    last, first = rims(query_feats, key_feats, value_feats, out_grad)
+    before = shifted(last, "ctx", 1)
+    following = shifted(first, "ctx", -1)
     x, qc, kc, vc = featurize(query_feats, key_feats, value_feats, out_grad, before, taps_full, long_filter.T, n_ctx)
     x = lax.all_to_all(x, "ctx", 0, 0, tiled=True)
     y = longconv(x, 1.0 / math.sqrt(length))
     y = lax.all_to_all(y, "ctx", 0, 0, tiled=True)
-    after = shifted(heads(y, qc, kc, vc, out_grad, skip), "ctx", -1)
-    mixed_out, gq, gk, gv, rims, gf = spread(y, qc, kc, vc, out_grad, skip, taps_full)
-    gq, gk, gv = tail(rims, after, taps_full, gq, gk, gv)
+    mixed_out, gq, gk, gv, gf = spread(y, qc, kc, vc, out_grad, skip, taps_full, last, following)
     return (mixed_out, gq, gk, gv, gf.T)
 
 

time: 117 us -> 112 us (0.957)
  the two profiles are of different devices: /device:TPU:38 before, /device:TPU:34 now
where the time goes in v5:
time: 112 us; the launch traced here: 111 us
  blocking collectives  49.1 us (44%)
  waiting for transfers between devices  25.4 us (23%)
  Pallas kernels  23.6 us (21%)
  starting transfers between devices  10.6 us (9%)
  local copies, waits for them, and re-layouts  1.91 us (2%)
    all_to_all x1, blocking collectives, body(): x = lax.all_to_all(x, 'ctx', 0, 0, tiled=True)  49.1 us
    all_to_all x1, waiting for transfers between devices, body(): y = lax.all_to_all(y, 'ctx', 0, 0, tiled=True)  17.3 us
    pallas_call x1, Pallas kernels, longconv(): pl.pallas_call(functools.partial(longconv_kernel, scale=scale), grid=(gro...  10.9 us
    ppermute x2, waiting for transfers between devices, shifted(): lax.ppermute(value, axis, [(source, source + steps) for source in range(i...  8.15 us
    pallas_call x1, Pallas kernels, spread(): pl.pallas_call(spread_kernel, grid=(width // cols,), in_specs=[resident]...  5.95 us
    pallas_call x1, Pallas kernels, featurize(): pl.pallas_call(featurize_kernel, grid=(width // cols,), in_specs=[tok, to...  5.85 us
    ppermute x2, starting transfers between devices, shifted(): lax.ppermute(value, axis, [(source, source + steps) for source in range(i...  5.66 us
    all_to_all x1, starting transfers between devices, body(): y = lax.all_to_all(y, 'ctx', 0, 0, tiled=True)  4.97 us
  transfers between devices with their start and end apart: 3, of which 3 were waited for; matrix products, arithmetic and copies ran while one was open for 1% of the time, Pallas kernels for 0%

profile of v5, /device:TPU:34, one launch (start us, length us, event | category | flops | bytes accessed | tf_op | source)
XLA Modules:
  0.0 111.4 jit_solution(15436536199351693824)
XLA Ops:
  0.6 0.0 copy-start.3
  0.6 0.9 rims.1
  1.5 0.0 copy-start.1
  1.5 3.4 %collective-permute-start = (bf16[3,8,1024]{2,1,0:T(8,128)(2,1)S(1)}, bf16[3,8,1024]{2,1,0:T(8,128)(2,1)S(1)}, u32[]{:S(2)}, u32[]{:S(2)}) collective-permute-start(bf16[3,8,1024]{2,1,0:T(8,128)(2,1)S(1)} %get-tuple-element.16.last_ref), channel_id=1, source_target_pairs={{0,8},{8,16},{16,24},{24,32},{32,40},{40,48},{48,56},{56,64},{64,7... | collective-permute-start | bytes 147464 | tf_op jit(solution)/shard_map/ppermute | solution.py:31
  4.9 0.0 copy-done.3
  5.0 0.3 broadcast_in_dim.3
  5.2 0.4 reshape_reshape.3.taps_ref
  5.6 1.9 %collective-permute-done.before_ref = bf16[3,8,1024]{2,1,0:T(8,128)(2,1)S(1)} collective-permute-done((bf16[3,8,1024]{2,1,0:T(8,128)(2,1)S(1)}, bf16[3,8,1024]{2,1,0:T(8,128)(2,1)S(1)}, u32[]{:S(2)}, u32[]{:S(2)}) %collective-permute-start) | collective-permute-done | bytes 49184 | tf_op jit(solution)/shard_map/ppermute | solution.py:31
  7.5 0.0 copy-done.1
  7.5 5.9 %featurize.1 = (bf16[32,136,128]{2,1,0:T(8,128)(2,1)}, f32[256,1024]{1,0:T(8,128)S(1)}, f32[256,1024]{1,0:T(8,128)S(1)}, f32[256,1024]{1,0:T(8,128)}) custom-call(bf16[256,1024]{1,0:T(8,128)(2,1)} %q_ref.1, bf16[256,1024]{1,0:T(8,128)(2,1)} %k_ref.1, bf16[256,1024]{1,0:T(8,128)(2,1)} %v_ref.1, bf16[256,1024]{1,0:T(8,128)(2,1)} %g_ref.3, ...), custom_call_target="tpu_custom_call" | custom-call | tf_op jit(solution)/shard_map/featurize/pallas_call | solution.py:140
  13.4 49.1 %all_to_all.10.x_ref = bf16[32,136,128]{2,1,0:T(8,128)(2,1)S(1)} all-to-all(bf16[32,136,128]{2,1,0:T(8,128)(2,1)} %get-tuple-element.17), channel_id=1, replica_groups=mesh['ctx'=32,'tp'=8] {'ctx'}, dimensions={0} | all-to-all | bytes 2228224 | tf_op jit(solution)/shard_map/all_to_all | solution.py:470
  62.5 10.9 %longconv.1 = bf16[32,136,128]{2,1,0:T(8,128)(2,1)} custom-call(bf16[32,136,128]{2,1,0:T(8,128)(2,1)S(1)} %all_to_all.10.x_ref), custom_call_target="tpu_custom_call" | custom-call | tf_op jit(solution)/shard_map/longconv/pallas_call | solution.py:325
  73.4 0.0 copy-start.2
  73.4 5.0 %all-to-all-start.1 = ((bf16[32,136,128]{2,1,0:T(8,128)(2,1)}), bf16[32,136,128]{2,1,0:T(8,128)(2,1)S(1)}, u32[]{:S(2)}, u32[]{:S(2)}) async-start(bf16[32,136,128]{2,1,0:T(8,128)(2,1)} %longconv.1), calls=%async_computation.1 | async-start | bytes 2228224 | tf_op jit(solution)/shard_map/all_to_all | solution.py:472
  78.4 2.3 %collective-permute-start.1 = (bf16[4,8,1024]{2,1,0:T(8,128)(2,1)S(1)}, bf16[4,8,1024]{2,1,0:T(8,128)(2,1)S(1)}, u32[]{:S(2)}, u32[]{:S(2)}) collective-permute-start(bf16[4,8,1024]{2,1,0:T(8,128)(2,1)S(1)} %get-tuple-element.21), channel_id=1, source_target_pairs={{8,0},{16,8},{24,16},{32,24},{40,32},{48,40},{56,48},{64,56},{72,6... | collective-permute-start | bytes 196616 | tf_op jit(solution)/shard_map/ppermute | solution.py:31
  80.6 6.3 %collective-permute-done.1.next_ref = bf16[4,8,1024]{2,1,0:T(8,128)(2,1)S(1)} collective-permute-done((bf16[4,8,1024]{2,1,0:T(8,128)(2,1)S(1)}, bf16[4,8,1024]{2,1,0:T(8,128)(2,1)S(1)}, u32[]{:S(2)}, u32[]{:S(2)}) %collective-permute-start.1) | collective-permute-done | bytes 65568 | tf_op jit(solution)/shard_map/ppermute | solution.py:31
  86.9 17.3 %all-to-all-done.1.y_ref = bf16[32,136,128]{2,1,0:T(8,128)(2,1)S(1)} async-done(((bf16[32,136,128]{2,1,0:T(8,128)(2,1)}), bf16[32,136,128]{2,1,0:T(8,128)(2,1)S(1)}, u32[]{:S(2)}, u32[]{:S(2)}) %all-to-all-start.1) | async-done | bytes 1114144 | tf_op jit(solution)/shard_map/all_to_all | solution.py:472
  104.2 0.0 copy-done.2
  104.2 0.0 copy-start
  104.2 1.2 %copy-done = f32[256,1024]{1,0:T(8,128)S(1)} copy-done((f32[256,1024]{1,0:T(8,128)S(1)}, f32[256,1024]{1,0:T(8,128)}, u32[]{:S(2)}) %copy-start) | copy-done | bytes 1048600
  105.4 6.0 %spread.1 = (bf16[256,1024]{1,0:T(8,128)(2,1)}, bf16[256,1024]{1,0:T(8,128)(2,1)}, bf16[256,1024]{1,0:T(8,128)(2,1)}, bf16[256,1024]{1,0:T(8,128)(2,1)}, bf16[64,256]{1,0:T(8,128)(2,1)}) custom-call(bf16[32,136,128]{2,1,0:T(8,128)(2,1)S(1)} %all-to-all-done.1.y_ref, f32[256,1024]{1,0:T(8,128)S(1)} %get-tuple-element.18.qc_ref, ...), custom_call_target="tpu_custom_call" | custom-call | flops 12000000 | bytes 8000000 | tf_op jit(solution)/shard_map/spread/pallas_call | solution.py:438
  (1 shorter events, 0.0 us)
Async XLA Ops:
  0.6 4.3 %copy-start.3 = (f32[3,7,64]{2,1,0:T(8,128)S(1)}, f32[3,7,64]{2,1,0:T(8,128)}, u32[]{:S(2)}) copy-start(f32[3,7,64]{2,1,0:T(8,128)} %param.10) | copy-start | bytes 16132
  1.5 6.0 %copy-start.1 = (bf16[256,64]{0,1:T(8,128)(2,1)S(1)}, bf16[256,64]{0,1:T(8,128)(2,1)}, u32[]{:S(2)}) copy-start(bf16[256,64]{0,1:T(8,128)(2,1)} %param.11) | copy-start | bytes 98308
  1.5 6.0 %collective-permute-start = (bf16[3,8,1024]{2,1,0:T(8,128)(2,1)S(1)}, bf16[3,8,1024]{2,1,0:T(8,128)(2,1)S(1)}, u32[]{:S(2)}, u32[]{:S(2)}) collective-permute-start(bf16[3,8,1024]{2,1,0:T(8,128)(2,1)S(1)} %get-tuple-element.16.last_ref), channel_id=1, source_target_pairs={{0,8},{8,16},{16,24},{24,32},{32,40},{40,48},{48,56},{56,64},{64,7... | collective-permute-start | bytes 147464 | tf_op jit(solution)/shard_map/ppermute | solution.py:31
  73.4 30.8 %copy-start.2 = (f32[1024]{0:T(1024)S(1)}, f32[1024]{0:T(1024)}, u32[]{:S(2)}) copy-start(f32[1024]{0:T(1024)} %param.12) | copy-start | bytes 12292
  73.4 30.8 %all-to-all-start.1 = ((bf16[32,136,128]{2,1,0:T(8,128)(2,1)}), bf16[32,136,128]{2,1,0:T(8,128)(2,1)S(1)}, u32[]{:S(2)}, u32[]{:S(2)}) async-start(bf16[32,136,128]{2,1,0:T(8,128)(2,1)} %longconv.1), calls=%async_computation.1 | async-start | bytes 2228224 | tf_op jit(solution)/shard_map/all_to_all | solution.py:472
  78.4 8.5 %collective-permute-start.1 = (bf16[4,8,1024]{2,1,0:T(8,128)(2,1)S(1)}, bf16[4,8,1024]{2,1,0:T(8,128)(2,1)S(1)}, u32[]{:S(2)}, u32[]{:S(2)}) collective-permute-start(bf16[4,8,1024]{2,1,0:T(8,128)(2,1)S(1)} %get-tuple-element.21), channel_id=1, source_target_pairs={{8,0},{16,8},{24,16},{32,24},{40,32},{48,40},{56,48},{64,56},{72,6... | collective-permute-start | bytes 196616 | tf_op jit(solution)/shard_map/ppermute | solution.py:31
  104.2 1.2 %copy-start = (f32[256,1024]{1,0:T(8,128)S(1)}, f32[256,1024]{1,0:T(8,128)}, u32[]{:S(2)}) copy-start(f32[256,1024]{1,0:T(8,128)} %get-tuple-element.20.vc_ref) | copy-start | bytes 3145732
